TPU v7x, 32 devices: a whole 2x2x4 slice. The times are simulated.
32 devices in a mesh: seq: 8 (over y, x, core), tp: 4 (over z).
Axes of the slice: x: 2, y: 2, z: 4, core: 2. Of those that a mesh axis runs over, the one named last changes fastest.
Arguments:
- stream: bfloat16 [16384, 1024], P(('seq', 'tp')), may hold values from -6 to 6
- segments: int32 [16384], replicated, may hold values from 0 to 63, never falling along the last dimension, each value on 1 to 1024 neighbouring positions
- skip_values: bfloat16 [16384, 512], P('seq', 'tp'), may hold values from -6 to 6
- first_gain: float32 [1024], replicated, may hold values from 0.5 to 1.5
- first_shift: float32 [1024], replicated, may hold values from -1.75 to 1.75
- query_weight: bfloat16 [1024, 1024], P(None, 'tp'), may hold values from -0.1875 to 0.1875
- query_bias: float32 [1024], P('tp'), may hold values from -3 to 3
- key_weight: bfloat16 [1024, 1024], P(None, 'tp'), may hold values from -0.1875 to 0.1875
- value_weight: bfloat16 [1024, 512], P(None, 'tp'), may hold values from -0.1875 to 0.1875
- value_bias: float32 [512], P('tp'), may hold values from -3 to 3
- mixing_weight: bfloat16 [1024, 1024], P('tp'), may hold values from -1.5 to 1.5
- mixing_bias: float32 [1024], replicated, may hold values from -1.75 to 1.75
- second_gain: float32 [1024], replicated, may hold values from 0.5 to 1.5
- second_shift: float32 [1024], replicated, may hold values from -1.75 to 1.75
- up_weight: bfloat16 [1024, 4096], P(None, 'tp'), may hold values from -0.1875 to 0.1875
- up_bias: float32 [4096], P('tp'), may hold values from -3 to 3
- down_weight: bfloat16 [4096, 1024], P('tp'), may hold values from -0.09375 to 0.09375
- down_bias: float32 [1024], replicated, may hold values from -1.75 to 1.75
- cotangent: bfloat16 [16384, 1024], P(('seq', 'tp')), may hold values from -6 to 6
Outputs:
- output: bfloat16 [16384, 1024], P(('seq', 'tp'))
- stream_gradient: float32 [16384, 1024], P(('seq', 'tp'))
- skip_gradient: float32 [16384, 512], P('seq', 'tp')
- query_gradient: float32 [1024, 1024], P('seq', 'tp')
- query_bias_gradient: float32 [1024], replicated
- key_gradient: float32 [1024, 1024], P('seq', 'tp')
- value_gradient: float32 [1024, 512], P('seq', 'tp')
- value_bias_gradient: float32 [512], replicated
- mixing_gradient: float32 [1024, 1024], P('tp', 'seq')
- mixing_bias_gradient: float32 [1024], replicated
- first_gain_gradient: float32 [1024], replicated
- first_shift_gradient: float32 [1024], replicated
- second_gain_gradient: float32 [1024], replicated
- second_shift_gradient: float32 [1024], replicated
- up_gradient: float32 [1024, 4096], P('seq', 'tp')
- up_bias_gradient: float32 [4096], replicated
- down_gradient: float32 [4096, 1024], P('tp', 'seq')
- down_bias_gradient: float32 [1024], replicated
Inputs may be any that keep to these rules, and one draw needn't show every extreme that they name: `segments`: segment numbers never fall along the stream; each document spans 1 to 1024 tokens, and some document spans exactly 1024.
All inputs are finite; a program needn't handle non-finite values.
Results may differ from a plain program's by a relative error of at most 0.012.
Values may be sent and summed in bfloat16 or wider, within the bound.
No kernel may reach another device: no remote copies, remote signals or barrier semaphores. Data moves between devices by JAX's collectives and lax.ppermute only.
A program may use at most 128 MiB of HBM per device.

v0:
```python
import functools

import jax
import jax.numpy as jnp
from jax import lax
from jax.experimental import pallas as pl
from jax.experimental.pallas import tpu as pltpu
from jax.sharding import PartitionSpec as P

HEAD = 64
DOC_MAX = 1024
PAIR = 2 * HEAD
TILE = 256
UNIT = 512
EPSILON = 1e-05
F32 = jnp.float32
BF16 = jnp.bfloat16
SCALE = HEAD ** -0.5
GELU_A = 0.7978845608028654
GELU_B = 0.044715
SEQ = ("run", "core")
GATHER_STEP = 1


def dot(a, b, dims, out=F32):
    return lax.dot_general(a, b, (dims, ((), ())), preferred_element_type=out)


def nn(a, b):
    return dot(a, b, ((1,), (0,)))


def nt(a, b):
    return dot(a, b, ((1,), (1,)))


def tn(a, b):
    return dot(a, b, ((0,), (0,)))


def light(bytes_accessed, flops=1):
    return pl.CostEstimate(flops=flops, bytes_accessed=bytes_accessed, transcendentals=0)


ANY = pl.BlockSpec(memory_space=pl.ANY)


def project_kernel(slot, place_ref, piece_ref, weight_ref, bias_ref, *rest):
    qkv_ref, turned_ref = rest[-2:]
    piece = piece_ref[...]
    qkv_ref[...] = (nn(piece, weight_ref[...]) + bias_ref[...]).astype(BF16)
    turned_ref[...] = piece.T


def project(k, count, place, piece, weight, bias, earlier):
    rows, width = piece.shape
    cols = weight.shape[1]
    slot = (count - k) % count
    tile = rows // 2
    alias = earlier is not None
    return pl.pallas_call(
        functools.partial(project_kernel, slot),
        grid_spec=pltpu.PrefetchScalarGridSpec(
            num_scalar_prefetch=1,
            grid=(2,),
            in_specs=[
                pl.BlockSpec((tile, width), lambda i, p: (i, 0)),
                pl.BlockSpec((width, cols), lambda i, p: (0, 0)),
                pl.BlockSpec((1, cols), lambda i, p: (0, 0)),
            ]
            + ([ANY, ANY] if alias else []),
            out_specs=[
                pl.BlockSpec((tile, cols), lambda i, p: (2 * lax.rem(p[0] + slot, count) + i, 0)),
                pl.BlockSpec((width, tile), lambda i, p: (0, 2 * slot + i)),
            ],
        ),
        out_shape=[
            jax.ShapeDtypeStruct((count * rows, cols), BF16),
            jax.ShapeDtypeStruct((width, count * rows), BF16),
        ],
        input_output_aliases={4: 0, 5: 1} if alias else {},
        cost_estimate=light(4 * rows * width, 2 * rows * width * cols),
        name="project",
    )(place, piece, weight, bias, *(earlier if alias else ()))


def turn_kernel(own_ref, got_ref, out_ref):
    rows = own_ref.shape[0]
    out_ref[:, :rows] = own_ref[...].T
    out_ref[:, rows:] = got_ref[...].T


def turn_rows(own, got):
    rows, width = own.shape
    tile = width // 4
    return pl.pallas_call(
        turn_kernel,
        grid=(4,),
        in_specs=[pl.BlockSpec((rows, tile), lambda i: (0, i))] * 2,
        out_specs=pl.BlockSpec((tile, 2 * rows), lambda i: (i, 0)),
        out_shape=jax.ShapeDtypeStruct((width, 2 * rows), BF16),
        cost_estimate=light(8 * rows * width),
        name="turn_rows",
    )(own, got)


def wide(tile):
    lane = lax.broadcasted_iota(jnp.int32, tile.shape, 1)
    zero = jnp.zeros_like(tile)
    return jnp.concatenate(
        (jnp.where(lane < HEAD, tile, zero), jnp.where(lane < HEAD, zero, tile)), axis=0
    )


def both(row):
    return jnp.concatenate((row, row), axis=1)


def heads_of(acc):
    return jnp.concatenate((acc[:HEAD, :TILE], acc[HEAD:, TILE:]), axis=0)


def mask_rows(start_ref, step, shift):
    start = both(start_ref[...] - shift)
    place = both((step + 4) * TILE + lax.broadcasted_iota(jnp.int32, (1, TILE), 1))
    return start, place


def allowed(tile_index, start, place):
    key = tile_index * TILE + lax.broadcasted_iota(jnp.int32, (TILE, 2 * TILE), 0)
    return (key >= start) & (key <= place)


def turn(tile, meta_ref, tiles, per, count):
    block = tile // per
    return per * lax.rem(block - meta_ref[tiles] + count, count) + lax.rem(tile, per)


def attend_kernel(base, shift, meta_ref, start_ref, q_ref, k_ref, v_ref, *rest):
    o_ref, turned_ref, log_ref, acc_ref = rest[-4:]
    step = pl.program_id(0)
    query = wide(q_ref[...] * jnp.asarray(SCALE, BF16))
    start, place = mask_rows(start_ref, step, shift)
    acc_ref[...] = jnp.zeros_like(acc_ref)

    def body(j, carried):
        top, total = carried
        rows = pl.ds(pl.multiple_of(j * TILE, TILE), TILE)
        scores = nt(k_ref[rows, :], query)
        scores = jnp.where(allowed(j, start, place), scores, -1e30)
        new_top = jnp.maximum(top, jnp.max(scores, axis=0, keepdims=True))
        part = jnp.exp(scores - new_top)
        factor = jnp.exp(top - new_top)
        total = total * factor + jnp.sum(part, axis=0, keepdims=True)
        acc_ref[...] = acc_ref[...] * factor + tn(v_ref[rows, :], part.astype(BF16))
        return new_top, total

    top, total = lax.fori_loop(
        meta_ref[base + step] - shift // TILE,
        step + 5,
        body,
        (jnp.full((1, 2 * TILE), -1e30, F32), jnp.zeros((1, 2 * TILE), F32)),
    )
    turned = heads_of(acc_ref[...] / total)
    turned_ref[...] = turned
    o_ref[...] = turned.T.astype(BF16)
    logs = top + jnp.log(total)
    log_ref[0:1, :] = logs[:, :TILE]
    log_ref[1:2, :] = logs[:, TILE:]


def attend(base, shift, meta, start, q, qcol, k, kcol, v, vcol, earlier, tokens, count):
    n = k.shape[0]
    steps = (n - DOC_MAX) // TILE
    tiles = tokens // TILE
    per = tiles // count
    alias = earlier is not None
    specs = [
        pl.BlockSpec((1, TILE), lambda i, m: (0, base + i)),
        pl.BlockSpec((TILE, PAIR), lambda i, m: (base + i, qcol)),
        pl.BlockSpec((n, PAIR), lambda i, m: (0, kcol)),
        pl.BlockSpec((n, PAIR), lambda i, m: (0, vcol)),
    ] + [ANY] * (3 if alias else 0)
    return pl.pallas_call(
        functools.partial(attend_kernel, base, shift),
        grid_spec=pltpu.PrefetchScalarGridSpec(
            num_scalar_prefetch=1,
            grid=(steps,),
            in_specs=specs,
            out_specs=[
                pl.BlockSpec((TILE, PAIR), lambda i, m: (turn(base + i, m, tiles, per, count), 0)),
                pl.BlockSpec((PAIR, TILE), lambda i, m: (0, base + i)),
                pl.BlockSpec((8, TILE), lambda i, m: (0, base + i)),
            ],
            scratch_shapes=[pltpu.VMEM((PAIR, 2 * TILE), F32)],
        ),
        out_shape=[
            jax.ShapeDtypeStruct((tokens, PAIR), BF16),
            jax.ShapeDtypeStruct((PAIR, tokens), F32),
            jax.ShapeDtypeStruct((8, tokens), F32),
        ],
        input_output_aliases={5: 0, 6: 1, 7: 2} if alias else {},
        cost_estimate=light(4 * n * PAIR),
        name="attend",
    )(meta, start, q, k, v, *(earlier if alias else ()))


def back_tile(shift, low, start_ref, q_ref, k_ref, v_ref, do_ref, turned_ref, log_ref, dk_ref, dv_ref, acc_ref):
    step = pl.program_id(0)
    query = wide(q_ref[...] * jnp.asarray(SCALE, BF16))
    out_back = wide(do_ref[...])
    start, place = mask_rows(start_ref, step, shift)
    product = do_ref[...].astype(F32).T * turned_ref[...]
    delta = jnp.concatenate(
        (
            jnp.sum(product[:HEAD], axis=0, keepdims=True),
            jnp.sum(product[HEAD:], axis=0, keepdims=True),
        ),
        axis=1,
    )
    logs = jnp.concatenate((log_ref[0:1, :], log_ref[1:2, :]), axis=1)
    acc_ref[...] = jnp.zeros_like(acc_ref)

    def body(j, carried):
        rows = pl.ds(pl.multiple_of(j * TILE, TILE), TILE)
        key_tile = k_ref[rows, :]
        scores = jnp.where(allowed(j, start, place), nt(key_tile, query), -1e30)
        prob = jnp.exp(scores - logs)
        prob_back = nt(v_ref[rows, :], out_back)
        score_back = (prob * (prob_back - delta)).astype(BF16)
        dv_ref[rows, :] += nn(prob.astype(BF16), out_back)
        dk_ref[rows, :] += nn(score_back, query)
        acc_ref[...] += tn(key_tile, score_back)
        return carried

    lax.fori_loop(low, step + 5, body, 0)
    return (heads_of(acc_ref[...]) * SCALE).T.astype(BF16)


def early_kernel(meta_ref, start_ref, q_ref, k_ref, v_ref, do_ref, turned_ref, log_ref, dq_ref, gone_ref, dk_ref, dv_ref, kept_k, kept_v, acc_ref):
    step = pl.program_id(0)

    @pl.when(step == 0)
    def _():
        kept_k[...] = jnp.zeros_like(kept_k)
        kept_v[...] = jnp.zeros_like(kept_v)

    dq_ref[...] = back_tile(
        0, meta_ref[step], start_ref, q_ref, k_ref, v_ref, do_ref, turned_ref, log_ref,
        kept_k, kept_v, acc_ref,
    )

    @pl.when(step == pl.num_programs(0) - 1)
    def _():
        gone_ref[:, :PAIR] = kept_k[:DOC_MAX, :].astype(BF16)
        gone_ref[:, PAIR:] = kept_v[:DOC_MAX, :].astype(BF16)
        dk_ref[...] = kept_k[DOC_MAX:, :]
        dv_ref[...] = kept_v[DOC_MAX:, :]


def late_kernel(base, fresh, per, count, meta_ref, start_ref, q_ref, k_ref, v_ref, do_ref, turned_ref, log_ref, dq_in, dk_in, dv_in, back_ref, packed_ref, value_ref, sums_ref, kept_k, kept_v, acc_ref):
    step = pl.program_id(0)
    held = dk_in.shape[0]
    tiles = packed_ref.shape[0] // TILE

    def rows_of(tile):
        row = turn(tile, meta_ref, tiles, per, count) * TILE
        return pl.ds(pl.multiple_of(row, TILE), TILE)

    @pl.when(step == 0)
    def _():
        kept_k[:held, :] = dk_in[...]
        kept_v[:held, :] = dv_in[...]
        kept_k[held:, :] = back_ref[:, :PAIR].astype(F32)
        kept_v[held:, :] = back_ref[:, PAIR:].astype(F32)
        for i in range(base):
            packed_ref[rows_of(i), :PAIR] = dq_in[i * TILE : (i + 1) * TILE, :]

    packed_ref[rows_of(base + step), :PAIR] = back_tile(
        DOC_MAX, meta_ref[base + step] - DOC_MAX // TILE, start_ref, q_ref, k_ref, v_ref, do_ref,
        turned_ref, log_ref, kept_k, kept_v, acc_ref,
    )

    @pl.when(step == pl.num_programs(0) - 1)
    def _():
        for i in range(tiles):
            span = slice(i * TILE, (i + 1) * TILE)
            packed_ref[rows_of(i), PAIR : 2 * PAIR] = kept_k[span, :].astype(BF16)
            if fresh:
                packed_ref[rows_of(i), 2 * PAIR :] = kept_v[span, :].astype(BF16)
        if not fresh:
            value_ref[...] = kept_v[...]
        else:
            value_ref[...] = jnp.zeros_like(value_ref)
        sums_ref[...] = jnp.broadcast_to(
            jnp.sum(packed_ref[...].astype(F32), axis=0, keepdims=True), sums_ref.shape
        )


def back_specs(base, qcol, n, kcol, vcol, tiles, per, count):
    return [
        pl.BlockSpec((1, TILE), lambda i, m: (0, base + i)),
        pl.BlockSpec((TILE, PAIR), lambda i, m: (base + i, qcol)),
        pl.BlockSpec((n, PAIR), lambda i, m: (0, kcol)),
        pl.BlockSpec((n, PAIR), lambda i, m: (0, vcol)),
        pl.BlockSpec((TILE, PAIR), lambda i, m: (turn(base + i, m, tiles, per, count), 0)),
        pl.BlockSpec((PAIR, TILE), lambda i, m: (0, base + i)),
        pl.BlockSpec((8, TILE), lambda i, m: (0, base + i)),
    ]


def whole(shape):
    return pl.BlockSpec(shape, lambda i, m: (0,) * len(shape))


def back_early(meta, start, q, qcol, k, kcol, v, vcol, do, turned, logs, tokens, count):
    n = k.shape[0]
    held = n - DOC_MAX
    tiles = tokens // TILE
    return pl.pallas_call(
        early_kernel,
        grid_spec=pltpu.PrefetchScalarGridSpec(
            num_scalar_prefetch=1,
            grid=(held // TILE,),
            in_specs=back_specs(0, qcol, n, kcol, vcol, tiles, tiles // count, count),
            out_specs=[
                pl.BlockSpec((TILE, PAIR), lambda i, m: (i, 0)),
                whole((DOC_MAX, 2 * PAIR)),
                whole((held, PAIR)),
                whole((held, PAIR)),
            ],
            scratch_shapes=[
                pltpu.VMEM((n, PAIR), F32),
                pltpu.VMEM((n, PAIR), F32),
                pltpu.VMEM((PAIR, 2 * TILE), F32),
            ],
        ),
        out_shape=[
            jax.ShapeDtypeStruct((held, PAIR), BF16),
            jax.ShapeDtypeStruct((DOC_MAX, 2 * PAIR), BF16),
            jax.ShapeDtypeStruct((held, PAIR), F32),
            jax.ShapeDtypeStruct((held, PAIR), F32),
        ],
        cost_estimate=light(12 * n * PAIR),
        name="back_early",
    )(meta, start, q, k, v, do, turned, logs)


def back_late(meta, start, q, qcol, k, kcol, v, vcol, do, turned, logs, dq, dk, dv, back, fresh, tokens, count):
    n = k.shape[0]
    held = n - DOC_MAX
    tiles = tokens // TILE
    per = tiles // count
    base = (tokens - held) // TILE
    cols = (3 if fresh else 2) * PAIR
    return pl.pallas_call(
        functools.partial(late_kernel, base, fresh, per, count),
        grid_spec=pltpu.PrefetchScalarGridSpec(
            num_scalar_prefetch=1,
            grid=(held // TILE,),
            in_specs=back_specs(base, qcol, n, kcol, vcol, tiles, per, count)
            + [whole(dq.shape), whole(dk.shape), whole(dv.shape), whole(back.shape)],
            out_specs=[
                whole((tokens, cols)),
                whole((8, PAIR) if fresh else (tokens, PAIR)),
                whole((8, cols)),
            ],
            scratch_shapes=[
                pltpu.VMEM((n, PAIR), F32),
                pltpu.VMEM((n, PAIR), F32),
                pltpu.VMEM((PAIR, 2 * TILE), F32),
            ],
        ),
        out_shape=[
            jax.ShapeDtypeStruct((tokens, cols), BF16),
            jax.ShapeDtypeStruct((8, PAIR) if fresh else (tokens, PAIR), F32),
            jax.ShapeDtypeStruct((8, cols), F32),
        ],
        cost_estimate=light(12 * n * PAIR),
        name="back_late",
    )(meta, start, q, k, v, do, turned, logs, dq, dk, dv, back)


def store_grad(grad_ref, grad):
    runs, _, lanes, rows, cols = grad_ref.shape
    for j in range(lanes):
        grad_ref[:, 0, j] = grad[:, j * cols : (j + 1) * cols].reshape(runs, rows, cols)


def accumulate(ref, value):
    @pl.when(pl.program_id(0) == 0)
    def _():
        ref[...] = value

    @pl.when(pl.program_id(0) > 0)
    def _():
        ref[...] += value


def up_kernel(places_ref, sn_ref, got_ref, cot_ref, up_ref, bias_ref, down_ref, out_ref, other_ref, slope_ref, grad_ref, act_ref):
    width = up_ref.shape[0] * up_ref.shape[1]
    rows = sn_ref.shape[0]
    up = up_ref[...].reshape(width, UNIT)
    down = down_ref[...].reshape(UNIT, width)
    for i, (piece_ref, sum_ref) in enumerate(((sn_ref, out_ref), (got_ref, other_ref))):
        span = slice(i * rows, (i + 1) * rows)
        hidden = nn(piece_ref[...], up) + bias_ref[0]
        square = hidden * hidden
        curve = jnp.tanh(GELU_A * (hidden + GELU_B * (hidden * square)))
        half = 0.5 * (1.0 + curve)
        activated = (hidden * half).astype(BF16)
        slope_ref[span, :] = half + 0.5 * hidden * (1.0 - curve * curve) * (
            GELU_A * (1.0 + 3.0 * GELU_B * square)
        )
        act_ref[span, :] = activated
        accumulate(sum_ref, nn(activated, down))
    store_grad(grad_ref, nn(cot_ref[...], act_ref[...]).astype(BF16))


def feed_specs(gathered, seq, parts, width):
    part = width // seq
    per = width // UNIT
    run = seq // 2

    def spot(i, p):
        return lax.rem(p[0] + i, parts)

    grad_spec = pl.BlockSpec(
        (run, 1, UNIT // PAIR, width // run, PAIR), lambda i, p: (0, i, 0, 0, 0)
    )

    grad = (run, parts, UNIT // PAIR, width // run, PAIR)
    return (
        pl.BlockSpec((seq, part, UNIT), lambda i, p: (spot(i, p), 0, p[1])),
        pl.BlockSpec((UNIT // part, part, width), lambda i, p: (spot(i, p) * per + p[1], 1, 0)),
        grad_spec,
        grad,
    )


def fixed(shape):
    return pl.BlockSpec(shape, lambda i, p: (0,) * len(shape))


def feed_up(places, sn, got, cot_turned, gathered, bias, seq, parts):
    rows, width = sn.shape
    up_spec, down_spec, grad_spec, grad = feed_specs(gathered, seq, parts, width)
    return pl.pallas_call(
        up_kernel,
        grid_spec=pltpu.PrefetchScalarGridSpec(
            num_scalar_prefetch=1,
            grid=(parts,),
            in_specs=[
                fixed((rows, width)),
                fixed((rows, width)),
                fixed((width, 2 * rows)),
                up_spec,
                pl.BlockSpec((1, 1, UNIT), lambda i, p: (lax.rem(parts - i, parts), 0, p[1])),
                down_spec,
            ],
            out_specs=[
                fixed((rows, width)),
                fixed((rows, width)),
                pl.BlockSpec((2 * rows, UNIT), lambda i, p: (0, i)),
                grad_spec,
            ],
            scratch_shapes=[pltpu.VMEM((2 * rows, UNIT), BF16)],
        ),
        out_shape=[
            jax.ShapeDtypeStruct((rows, width), F32),
            jax.ShapeDtypeStruct((rows, width), F32),
            jax.ShapeDtypeStruct((2 * rows, parts * UNIT), F32),
            jax.ShapeDtypeStruct(grad, BF16),
        ],
        cost_estimate=light(16 * rows * width, 24 * rows * width * width),
        name="feed_up",
    )(places, sn, got, cot_turned, gathered, bias, gathered)


def down_kernel(places_ref, cot_ref, cot_got_ref, sn_ref, got_ref, slope_ref, up_ref, down_ref, back_ref, other_ref, grad_ref, bias_ref, turned_ref, hidden_ref):
    width = up_ref.shape[0] * up_ref.shape[1]
    rows = sn_ref.shape[0]

    @pl.when(pl.program_id(0) == 0)
    def _():
        turned_ref[:, :rows] = sn_ref[...].T
        turned_ref[:, rows:] = got_ref[...].T

    up = up_ref[...].reshape(width, UNIT)
    down = down_ref[...].reshape(UNIT, width)
    total = jnp.zeros((1, UNIT), F32)
    for i, (piece_ref, sum_ref) in enumerate(((cot_ref, back_ref), (cot_got_ref, other_ref))):
        span = slice(i * rows, (i + 1) * rows)
        rounded = (nt(piece_ref[...], down) * slope_ref[span, :]).astype(BF16)
        total = total + jnp.sum(rounded.astype(F32), axis=0, keepdims=True)
        hidden_ref[span, :] = rounded
        accumulate(sum_ref, nt(rounded, up))
    bias_ref[0] = total
    store_grad(grad_ref, nn(turned_ref[...], hidden_ref[...]).astype(BF16))


def feed_down(places, cot, cot_got, sn, got, slope, gathered, seq, parts, extra):
    rows, width = cot.shape
    up_spec, down_spec, grad_spec, grad = feed_specs(gathered, seq, parts, width)
    return pl.pallas_call(
        down_kernel,
        grid_spec=pltpu.PrefetchScalarGridSpec(
            num_scalar_prefetch=1,
            grid=(parts,),
            in_specs=[fixed((rows, width))] * 4
            + [
                pl.BlockSpec((2 * rows, UNIT), lambda i, p: (0, i)),
                up_spec,
                down_spec,
            ],
            out_specs=[
                fixed((rows, width)),
                fixed((rows, width)),
                grad_spec,
                pl.BlockSpec((1, 1, UNIT), lambda i, p: (i, 0, 0)),
            ],
            scratch_shapes=[
                pltpu.VMEM((width, 2 * rows), BF16),
                pltpu.VMEM((2 * rows, UNIT), BF16),
            ],
        ),
        out_shape=[
            jax.ShapeDtypeStruct((rows, width), F32),
            jax.ShapeDtypeStruct((rows, width), F32),
            jax.ShapeDtypeStruct(grad[:2] + (grad[2] + extra,) + grad[3:], BF16),
            jax.ShapeDtypeStruct((parts, 1, UNIT), F32),
        ],
        cost_estimate=light(16 * rows * width, 24 * rows * width * width),
        name="feed_down",
    )(places, cot, cot_got, sn, got, slope, gathered, gathered)


def back_norm_kernel(own_ref, came_ref, cot_ref, hat_ref, inverse_ref, gain_ref, mixing_ref, mixed_ref, grads_ref, middle_ref, attended_ref, sums_ref, grad_ref, wide_ref):
    step = pl.program_id(0)
    back = own_ref[...] + came_ref[...]
    hat = hat_ref[...]
    cot = cot_ref[...].astype(F32)
    middle_back = cot + norm_back(back, gain_ref[...], hat, inverse_ref[...])
    rounded = middle_back.astype(BF16)
    middle_ref[...] = middle_back
    attended = nt(rounded, mixing_ref[...]).astype(BF16)
    for j in range(attended_ref.shape[0]):
        attended_ref[j] = attended[:, j * PAIR : (j + 1) * PAIR]
    accumulate(wide_ref, nn(rounded.T, mixed_ref[...]))

    @pl.when(step == 0)
    def _():
        sums_ref[...] = jnp.zeros_like(sums_ref)

    for i, value in enumerate((back * hat, back, middle_back, cot)):
        sums_ref[i : i + 1, :] += jnp.sum(value, axis=0, keepdims=True)

    @pl.when(step == pl.num_programs(0) - 1)
    def _():
        runs, parts, lanes, rows, cols = grad_ref.shape
        for k in range(parts):
            for j in range(lanes):
                left = (k * lanes + j) * cols
                value = wide_ref[:, left : left + cols].astype(BF16)
                grad_ref[:, (parts - k) % parts, j] = value.reshape(runs, rows, cols)


def back_norm(own, came, cot, hat, inverse, gain, mixing, mixed, grads):
    rows, width = own.shape
    blocks = mixing.shape[0] // PAIR
    runs, parts, lanes, lines, cols = grads.shape
    extra = blocks // parts
    tile = rows // 2
    row = pl.BlockSpec((tile, width), lambda i: (i, 0))
    return pl.pallas_call(
        back_norm_kernel,
        grid=(2,),
        in_specs=[
            row, row, row, row,
            pl.BlockSpec((tile, 1), lambda i: (i, 0)),
            pl.BlockSpec((1, width), lambda i: (0, 0)),
            pl.BlockSpec(mixing.shape, lambda i: (0, 0)),
            row,
            ANY,
        ],
        out_specs=[
            row,
            pl.BlockSpec((blocks, tile, PAIR), lambda i: (0, i, 0)),
            pl.BlockSpec((8, width), lambda i: (0, 0)),
            pl.BlockSpec((runs, parts, extra, lines, cols), lambda i: (0, 0, UNIT // PAIR // extra, 0, 0)),
        ],
        out_shape=[
            jax.ShapeDtypeStruct((rows, width), F32),
            jax.ShapeDtypeStruct((blocks, rows, PAIR), BF16),
            jax.ShapeDtypeStruct((8, width), F32),
            jax.ShapeDtypeStruct(grads.shape, BF16),
        ],
        input_output_aliases={8: 3},
        scratch_shapes=[pltpu.VMEM((width, width), F32)],
        cost_estimate=light(16 * rows * width, 4 * rows * width * width),
        name="back_norm",
    )(own, came, cot, hat, inverse, gain[None], mixing, mixed, grads)


def front_norm_kernel(parts, places_ref, *refs):
    pieces, (weight_ref, middle_ref, hat_ref, inverse_ref, gain_ref, out_ref) = refs[:-6], refs[-6:]
    cut = pieces[0].shape[1]
    back = jnp.zeros(out_ref.shape, F32)
    for k in range(parts):
        spot = lax.rem(places_ref[0] - k + parts, parts)
        back = back + nn(pieces[2 * k][...], weight_ref[spot, :cut, :])
        back = back + nn(pieces[2 * k + 1][...], weight_ref[spot, cut:, :])
    out_ref[...] = middle_ref[...] + norm_back(
        back, gain_ref[...], hat_ref[...], inverse_ref[...]
    )


def front_norm(places, pieces, weight, middle, hat, inverse, gain):
    rows, width = middle.shape
    parts = weight.shape[0]
    tile = rows // 4

    def row(cols):
        return pl.BlockSpec((tile, cols), lambda i, p: (i, 0))

    return pl.pallas_call(
        functools.partial(front_norm_kernel, parts),
        grid_spec=pltpu.PrefetchScalarGridSpec(
            num_scalar_prefetch=1,
            grid=(4,),
            in_specs=[row(piece.shape[1]) for piece in pieces]
            + [fixed(weight.shape), row(width), row(width), row(1), fixed((1, width))],
            out_specs=row(width),
        ),
        out_shape=jax.ShapeDtypeStruct((rows, width), F32),
        cost_estimate=light(16 * rows * width, 2 * rows * width * weight.shape[0] * weight.shape[1]),
        name="front_norm",
    )(places, *pieces, weight, middle, hat, inverse, gain[None])


def around(value, steps):
    count = lax.axis_size("tp")
    return lax.ppermute(value, "tp", [(i, (i + steps) % count) for i in range(count)])


def flipped(value, axis, bit):
    count = lax.axis_size(axis)
    return lax.ppermute(value, axis, [(i, i ^ bit) for i in range(count)])


def along(value, steps):
    count = lax.axis_size(SEQ)
    first, last = max(0, -steps), min(count, count - steps)
    return lax.ppermute(value, SEQ, [(i, i + steps) for i in range(first, last)])


def butterfly(value, axis):
    bit = 1
    while bit < lax.axis_size(axis):
        value = value + flipped(value, axis, bit)
        bit *= 2
    return value


def pick(value, index, dim):
    return lax.dynamic_index_in_dim(value, index, dim, keepdims=False)


def joined(a, b):
    return (a.astype(F32) + b.astype(F32)).astype(BF16)


def seq_bits():
    bits, bit = [], 1
    while bit < lax.axis_size(SEQ):
        bits.append(bit)
        bit *= 2
    return bits


def tied(*groups):
    return lax.optimization_barrier(groups)


class Scatter:
    def __init__(self, value, place):
        self.place = place
        self.bits = seq_bits()
        self.left = value.reshape((2,) * len(self.bits) + value.shape[1:])
        self.issue()

    def issue(self):
        bit = self.bits.pop(0)
        dim = len(self.bits)
        mine = (self.place // bit) % 2
        self.parts = (
            pick(self.left, mine, dim), flipped(pick(self.left, 1 - mine, dim), SEQ, bit)
        )

    def merge(self):
        self.left = joined(*self.parts)
        if self.bits:
            self.issue()
            return True
        return False

    def result(self):
        while self.merge():
            pass
        return self.left


def in_order(own, other, bit, place, dim):
    low = (place // bit) % 2 == 0
    return jnp.stack((jnp.where(low, own, other), jnp.where(low, other, own)), axis=dim)


def quarter(shard, place):
    size = shard.shape[0] // 4
    spot = 2 * ((place // 2) % 2) + place % 2
    return lax.dynamic_slice_in_dim(shard, spot * size, size, 0)


def from_shards(piece):
    return [around(piece, k) for k in range(1, lax.axis_size("tp"))]


def center(rows):
    average = jnp.mean(rows, axis=-1, keepdims=True)
    centered = rows - average
    inverse = lax.rsqrt(jnp.mean(centered * centered, axis=-1, keepdims=True) + EPSILON)
    return centered * inverse, inverse


def norm_back(grad, gain, xhat, inverse):
    e = grad * gain
    return inverse * (
        e
        - jnp.mean(e, axis=-1, keepdims=True)
        - xhat * jnp.mean(e * xhat, axis=-1, keepdims=True)
    )


def local(
    stream, segments, skip_values, first_gain, first_shift, query_weight, query_bias, key_weight,
    value_weight, value_bias, mixing_weight, mixing_bias, second_gain, second_shift, up_weight,
    up_bias, down_weight, down_bias, cotangent,
):
    rows, width = stream.shape
    tokens = skip_values.shape[0]
    own = query_weight.shape[1]
    tp = lax.axis_size("tp")
    seq = lax.axis_size(SEQ)
    seq_place = lax.axis_index(SEQ)
    tp_place = lax.axis_index("tp")
    core = lax.axis_index("core")
    places = jnp.stack((tp_place, core)).astype(jnp.int32)
    half = tokens - DOC_MAX
    part = width // seq
    kcol = own // PAIR

    stream_wide = stream.astype(F32)
    first_hat, first_inverse = center(stream_wide)
    piece = (first_hat * first_gain + first_shift).astype(BF16)
    piece, up_weight, down_weight, mixing_weight, segments, cotangent = lax.optimization_barrier(
        (piece, up_weight, down_weight, mixing_weight, segments, cotangent)
    )

    def own_rows(shard):
        size = shard.shape[0] // seq
        return lax.dynamic_slice_in_dim(shard, seq_place * size, size, 0)

    qkv_turned = jnp.concatenate(
        (
            query_weight[:, :PAIR], key_weight[:, :PAIR], value_weight,
            query_weight[:, PAIR:], key_weight[:, PAIR:],
        ),
        axis=1,
    ).T
    packet = jnp.concatenate([own_rows(w) for w in (up_weight, down_weight)], axis=0)
    qkv_packet = own_rows(qkv_turned)
    bias_pieces = jnp.stack([up_bias] + [around(up_bias, k) for k in range(1, tp)])[:, None]
    cot_got = flipped(cotangent, "core", 1)

    padded = jnp.concatenate((jnp.full((DOC_MAX,), -1, jnp.int32), segments))
    window = lax.dynamic_slice_in_dim(padded, seq_place * tokens, DOC_MAX + tokens, 0)
    start = jnp.sum(
        (window[:, None] < window[None, DOC_MAX:]).astype(jnp.int32), axis=0, keepdims=True
    )
    meta = jnp.concatenate((start[0, ::TILE] // TILE, places))
    halo_skip = along(skip_values[half:], 1)
    wqkv = jnp.concatenate((query_weight, key_weight, value_weight), axis=1)
    bias = jnp.concatenate((query_bias, jnp.zeros((own,), F32), value_bias))[None]
    made = None
    for k in range(tp):
        if k == tp - 1:
            piece, meta, start, bias_pieces, cot_got, mixing_piece = tied(
                piece, meta, start, bias_pieces, cot_got, quarter(mixing_weight, seq_place)
            )
        elif k > 0:
            piece, made = tied(piece, made)
        ahead = around(piece, 1) if k < tp - 1 else None
        made = project(k, tp, places, piece, wqkv, bias, made)
        piece = ahead
        if k == GATHER_STEP:
            piece, packet = tied(piece, packet)
            gathered = lax.all_gather(packet, ("tp",) + SEQ, axis=0, tiled=False)
    qkv, normed_turned = made
    halo = along(qkv[half:, own:], 1)
    qkv, mixing_piece = tied(qkv, mixing_piece)
    mixing_got = from_shards(mixing_piece)
    early = early_skip = None

    def values_of(pair):
        if pair == 0:
            return (qkv, 2 * kcol), (early, kcol)
        return (skip_values, 0), (early_skip, 0)

    steps = half // TILE
    attended = []
    for pair in range(2):
        (v, vcol), _ = values_of(pair)
        attended.append(
            attend(steps, DOC_MAX, meta, start, qkv, pair, qkv, kcol + pair, v, vcol, None, tokens, tp)
        )
    attended, halo, halo_skip, mixing_got = tied(attended, halo, halo_skip, mixing_got)
    early_skip = jnp.concatenate((halo_skip, skip_values[:half]), axis=0)
    early = jnp.concatenate((halo, qkv[:half, own:]), axis=0)
    mixing_got = jnp.stack(mixing_got)
    mixing_other = flipped(mixing_got, SEQ, 2)
    arrived = []
    for pair in range(2):
        _, (v, vcol) = values_of(pair)
        attended[pair] = attend(
            0, 0, meta, start, qkv, pair, early, pair, v, vcol, attended[pair], tokens, tp
        )
        blocks = attended[pair][0].reshape(tp, rows, PAIR)
        arrived.append([blocks[0]] + [around(blocks[k], k) for k in range(1, tp)])
    attended[1], mixing_got, mixing_other, cotangent, cot_got = tied(
        attended[1], mixing_got, mixing_other, cotangent, cot_got
    )
    mixing_got = in_order(mixing_got, mixing_other, 2, seq_place, 1)
    mixing_other = flipped(mixing_got, "core", 1)
    cot_turned = turn_rows(cotangent, cot_got)
    mixing_rot = in_order(mixing_got, mixing_other, 1, seq_place, 2).reshape(-1, width)
    mixing_rot = jnp.concatenate((mixing_weight, mixing_rot), axis=0)
    arrived, mixing_rot, cot_turned = tied(arrived, mixing_rot, cot_turned)

    mixed_in = jnp.concatenate([arrived[pair][k] for k in range(tp) for pair in range(2)], axis=1)
    middle = stream_wide + nn(mixed_in, mixing_rot) + mixing_bias
    second_hat, second_inverse = center(middle)
    second = (second_hat * second_gain + second_shift).astype(BF16)

    got = flipped(second, "core", 1)
    got, qkv_packet = tied(got, qkv_packet)
    qkv_full = lax.all_gather(qkv_packet, ("tp",) + SEQ, axis=0, tiled=False)
    qkv_full = qkv_full.reshape(tp, -1, width)
    lost, lost_other, slope, down_grads = feed_up(
        places, second, got, cot_turned, gathered, bias_pieces, seq, tp
    )

    def over_runs(grads):
        flat = grads.reshape(grads.shape[0], -1, PAIR)
        flat = lax.psum_scatter(flat, "run", scatter_dimension=0, tiled=True)
        return flat.reshape(grads.shape[1:])

    def over_shards(grads):
        return [grads[0]] + [around(grads[k], k) for k in range(1, tp)]

    down_grads = over_runs(down_grads)
    back_own, back_other, up_grads, up_bias_grad = feed_down(
        places, cotangent, cot_got, second, got, slope, gathered, seq, tp, UNIT // PAIR
    )
    back_came = flipped(back_other, "core", 1)
    middle_back, attended_back, norm_sums, up_grads = back_norm(
        back_own, back_came, cotangent, second_hat, second_inverse, second_gain, mixing_rot,
        mixed_in, up_grads,
    )
    up_grads = over_runs(up_grads)[:, : (UNIT + own) // PAIR]

    def send_back(pair):
        return [attended_back[pair]] + [
            around(attended_back[2 * k + pair], -k) for k in range(1, tp)
        ]

    moved = send_back(0)
    moved, attended_back, lost_other, qkv_full = tied(moved, attended_back, lost_other, qkv_full)
    returned = [jnp.concatenate(moved, axis=0)]
    moved = send_back(1)
    lost_came = flipped(lost_other, "core", 1)

    halves = []
    for pair in range(2):
        _, (v, vcol) = values_of(pair)
        _, turned, logs = attended[pair]
        dq, gone, dk, dv = back_early(
            meta, start, qkv, pair, early, pair, v, vcol, returned[pair], turned, logs, tokens, tp
        )
        halves.append((dq, dk, dv, along(gone, -1)))
        if pair == 0:
            dq, moved, lost_came = tied(dq, moved, lost_came)
            returned.append(jnp.concatenate(moved, axis=0))
    halves, norm_sums, up_bias_grad = tied(halves, norm_sums, up_bias_grad)
    halves = [list(group) for group in halves]
    made_here = [pick(up_bias_grad.reshape(tp, UNIT), (k - tp_place) % tp, 0) for k in range(tp)]
    made_here = jnp.stack(made_here).reshape(tp, 1, -1, PAIR)
    which = lax.broadcasted_iota(jnp.int32, (tp, 2) + made_here.shape[2:], 1)
    early_sums = jnp.concatenate(
        (
            norm_sums[:4].reshape(-1, PAIR),
            jnp.where(which == core, made_here, 0.0).reshape(-1, PAIR),
        ),
        axis=0,
    )
    packets, column_sums, pieces = [], [], []
    skip_gradient = None
    for pair in range(2):
        (v, vcol), _ = values_of(pair)
        _, turned, logs = attended[pair]
        packed, values, sums = back_late(
            meta, start, qkv, pair, qkv, kcol + pair, v, vcol, returned[pair], turned, logs,
            *halves[pair], pair == 0, tokens, tp,
        )
        blocks = packed.reshape(tp, rows, packed.shape[1])
        pieces.append([blocks[0]] + [around(blocks[k], k) for k in range(1, tp)])
        if pair == 0:
            halves[1], packed, down_grads = tied(halves[1], packed, down_grads)
            down_grads = over_shards(down_grads)
        else:
            skip_gradient = values
        packets.append(packed)
        column_sums.append(sums[0])
    packets, pieces[0], middle = tied(packets, pieces[0], middle)
    output = (middle + (lost + lost_came) + down_bias).astype(BF16)
    wide_grad = nn(normed_turned, jnp.concatenate(packets, axis=1))
    weight_sum = Scatter(wide_grad.astype(BF16).reshape(seq, part, -1), seq_place)
    pieces[1], weight_sum.parts, up_grads = tied(pieces[1], weight_sum.parts, up_grads)
    up_grads = over_shards(up_grads)
    weight_sum.merge()
    stream_gradient = front_norm(
        places, [pieces[pair][k] for k in range(tp) for pair in range(2)], qkv_full, middle_back,
        first_hat, first_inverse, first_gain,
    )
    column_sum = jnp.concatenate(column_sums)
    columns = qkv_turned.T.astype(F32)
    first_shift_part = jnp.sum(columns * column_sum, axis=1)
    hat_grad = (wide_grad - first_shift[:, None] * column_sum) / first_gain[:, None]
    first_gain_part = jnp.sum(columns * hat_grad, axis=1)

    def widen(value):
        size = value.shape[0]
        return lax.dynamic_update_slice_in_dim(
            jnp.zeros((size * tp,), F32), value, tp_place * size, 0
        )

    query_part = jnp.concatenate((column_sum[:PAIR], column_sum[3 * PAIR : 4 * PAIR]))
    late_sums = (
        first_gain_part, first_shift_part, widen(query_part),
        widen(column_sum[2 * PAIR : 3 * PAIR]),
    )
    late_sums = [value.reshape(-1, PAIR) for value in late_sums]
    sums = jnp.concatenate(late_sums + [early_sums], axis=0)
    for spot, bit in enumerate(seq_bits()):
        if spot + 1 < tp:
            sums, down_grads[spot + 1] = tied(sums, down_grads[spot + 1])
        sums = sums + flipped(sums, SEQ, bit)
    sums = butterfly(sums, "tp")
    weight_grad = weight_sum.result().astype(F32)

    def both_cores(blocks):
        cut = sum(block.astype(F32) for block in blocks)
        cut = cut.reshape(cut.shape[0], 2, part, PAIR)
        kept = pick(cut, core, 1)
        came = flipped(pick(cut, 1 - core, 1), "core", 1)
        lanes = UNIT // PAIR
        return jnp.concatenate(
            (
                jnp.where(core == 0, kept[:lanes], came[:lanes]),
                jnp.where(core == 0, came[:lanes], kept[:lanes]),
            ),
            axis=0,
        ), kept[lanes:] + came[lanes:]

    down_gradient = both_cores(down_grads)[0].transpose(0, 2, 1).reshape(-1, part)
    up_gradient, mixing_gradient = both_cores(up_grads)
    up_gradient = up_gradient.transpose(1, 0, 2).reshape(part, -1)
    mixing_gradient = mixing_gradient.transpose(0, 2, 1).reshape(-1, part)

    query_gradient = jnp.concatenate(
        (weight_grad[:, :PAIR], weight_grad[:, 3 * PAIR : 4 * PAIR]), axis=1
    )
    key_gradient = jnp.concatenate(
        (weight_grad[:, PAIR : 2 * PAIR], weight_grad[:, 4 * PAIR :]), axis=1
    )
    value_gradient = weight_grad[:, 2 * PAIR : 3 * PAIR]

    cuts = []
    for size in (width, width, width, width // 2) + (width,) * 4 + (tp * width,):
        cuts.append(sums[: size // PAIR].reshape(-1))
        sums = sums[size // PAIR :]
    (
        first_gain_grad, first_shift_grad, query_bias_grad, value_bias_grad, second_gain_grad,
        second_shift_grad, mixing_bias_grad, down_bias_grad, up_bias_grad,
    ) = cuts
    return (
        output,
        stream_gradient,
        skip_gradient,
        query_gradient,
        query_bias_grad,
        key_gradient,
        value_gradient,
        value_bias_grad,
        mixing_gradient,
        mixing_bias_grad,
        first_gain_grad,
        first_shift_grad,
        second_gain_grad,
        second_shift_grad,
        up_gradient,
        up_bias_grad,
        down_gradient,
        down_bias_grad,
    )


def solution(mesh):
    seq, tp = mesh.shape["seq"], mesh.shape["tp"]
    mesh = jax.sharding.Mesh(mesh.devices.reshape(seq // 2, 2, tp), SEQ + ("tp",))
    split = P(SEQ + ("tp",), None)
    column = P(None, "tp")
    tile = P(SEQ, "tp")
    turned = P("tp", SEQ)
    in_specs = (
        split, P(), tile, P(), P(), column, P("tp"), column, column, P("tp"),
        P("tp", None), P(), P(), P(), column, P("tp"), P("tp", None), P(), split,
    )
    out_specs = (
        split, split, tile, tile, P(), tile, tile, P(), turned, P(), P(), P(), P(), P(),
        tile, P(), turned, P(),
    )
    return jax.shard_map(local, mesh=mesh, in_specs=in_specs, out_specs=out_specs, check_vma=False)
```

profile of v0, /device:TPU:13, one launch (start us, length us, event | category | flops | bytes accessed | tf_op | source)
XLA Modules:
  0.0 530.7 jit_solution(5114233436736316223)
XLA Ops:
  10.5 2.1 fusion.6
  19.6 4.4 project.4
  23.9 13.1 %collective-permute-done.piece_ref = bf16[512,1024]{1,0:T(8,128)(2,1)} collective-permute-done((bf16[512,1024]{1,0:T(8,128)(2,1)}, bf16[512,1024]{1,0:T(8,128)(2,1)}, u32[]{:S(2)}, u32[]{:S(2)}) %collective-permute-start) | collective-permute-done | bytes 1048608 | tf_op jit(solution)/shard_map/ppermute | solution.py:643
  40.2 21.3 %collective-permute-done.1.piece_ref = bf16[512,1024]{1,0:T(8,128)(2,1)} collective-permute-done((bf16[512,1024]{1,0:T(8,128)(2,1)}, bf16[512,1024]{1,0:T(8,128)(2,1)}, u32[]{:S(2)}, u32[]{:S(2)}) %collective-permute-start.1) | collective-permute-done | bytes 1048608 | tf_op jit(solution)/shard_map/ppermute | solution.py:643
  61.9 4.7 collective-permute-start.4
  66.7 2.9 collective-permute-start.6
  69.6 4.3 project.5
  73.8 1.7 collective-permute-start.2
  75.6 2.5 convert_reduce_fusion
  80.4 4.3 project.6
  84.7 32.0 %collective-permute-done.2.piece_ref = bf16[512,1024]{1,0:T(8,128)(2,1)} collective-permute-done((bf16[512,1024]{1,0:T(8,128)(2,1)}, bf16[512,1024]{1,0:T(8,128)(2,1)}, u32[]{:S(2)}, u32[]{:S(2)}) %collective-permute-start.2) | collective-permute-done | bytes 1048608 | tf_op jit(solution)/shard_map/ppermute | solution.py:643
  116.7 4.4 project.7
  122.3 4.1 collective-permute-start.7
  126.5 1.9 collective-permute-start.8
  128.5 3.3 collective-permute-start.10
  133.3 7.8 %attend.5 = (bf16[2048,128]{1,0:T(8,128)(2,1)}, f32[128,2048]{1,0:T(8,128)}, f32[8,2048]{1,0:T(8,128)}) custom-call(s32[10]{0:T(128)} %pad_add_fusion.1.meta_ref, s32[1,2048]{1,0:T(1,128)} %bitcast.177, bf16[2048,640]{1,0:T(8,128)(2,1)} %get-tuple-element.186.q_ref.k_ref.v_ref, bf16[2048,640]{1,0:T(8,128)(2,1)} %get-tuple-element.186.q_ref.k_ref.v_ref, ...), custom_call_target="tpu_custom_call" | custom-call | flops 1 | bytes 1048576 | tf_op jit(solution)/shard_map/attend/pallas_call | solution.py:184
  141.1 7.8 %attend.4 = (bf16[2048,128]{1,0:T(8,128)(2,1)}, f32[128,2048]{1,0:T(8,128)}, f32[8,2048]{1,0:T(8,128)}) custom-call(s32[10]{0:T(128)} %pad_add_fusion.1.meta_ref, s32[1,2048]{1,0:T(1,128)} %bitcast.178, bf16[2048,640]{1,0:T(8,128)(2,1)} %get-tuple-element.186.q_ref.k_ref.v_ref, bf16[2048,640]{1,0:T(8,128)(2,1)} %get-tuple-element.186.q_ref.k_ref.v_ref, ...), custom_call_target="tpu_custom_call" | custom-call | flops 1 | bytes 1048576 | tf_op jit(solution)/shard_map/attend/pallas_call | solution.py:184
  151.1 2.4 pad_maximum_fusion.1.k_ref.v_ref
  153.5 7.3 %attend.6 = (bf16[2048,128]{1,0:T(8,128)(2,1)}, f32[128,2048]{1,0:T(8,128)}, f32[8,2048]{1,0:T(8,128)}) custom-call(s32[10]{0:T(128)} %pad_add_fusion.1.meta_ref, s32[1,2048]{1,0:T(1,128)} %bitcast.179, bf16[2048,640]{1,0:T(8,128)(2,1)} %get-tuple-element.186.q_ref.k_ref.v_ref, ...), custom_call_target="tpu_custom_call", output_to_operand_aliasing={{0}: (5, {}), {1}: (6, {}), {2}: (7, {})} | custom-call | flops 1 | bytes 1048576 | tf_op jit(solution)/shard_map/attend/pallas_call | solution.py:184
  160.8 7.0 %collective-permute-done.12 = bf16[3,64,1024]{2,1,0:T(8,128)(2,1)S(1)} collective-permute-done((bf16[3,64,1024]{2,1,0:T(8,128)(2,1)S(1)}, bf16[3,64,1024]{2,1,0:T(8,128)(2,1)S(1)}, u32[]{:S(2)}, u32[]{:S(2)}) %collective-permute-start.12) | collective-permute-done | bytes 393248 | tf_op jit(solution)/shard_map/ppermute | solution.py:648
  167.9 7.0 %collective-permute-start.19 = (bf16[3,2,64,1024]{3,2,0,1:T(8,128)(2,1)S(1)}, bf16[3,2,64,1024]{3,2,0,1:T(8,128)(2,1)}, u32[]{:S(2)}, u32[]{:S(2)}) collective-permute-start(bf16[3,2,64,1024]{3,2,0,1:T(8,128)(2,1)S(1)} %pad_maximum_fusion.3), channel_id=1, source_target_pairs={{0,4},{4,0},{1,5},{5,1},{2,6},{6,2},{3,7},{7,3},{8,12},{12,8},{9,1... | collective-permute-start | bytes 2359304 | tf_op jit(solution)/shard_map/ppermute | solution.py:648
  174.9 7.5 %attend.7 = (bf16[2048,128]{1,0:T(8,128)(2,1)}, f32[128,2048]{1,0:T(8,128)}, f32[8,2048]{1,0:T(8,128)}) custom-call(s32[10]{0:T(128)} %pad_add_fusion.1.meta_ref, s32[1,2048]{1,0:T(1,128)} %bitcast.180, bf16[2048,640]{1,0:T(8,128)(2,1)} %get-tuple-element.186.q_ref.k_ref.v_ref, ...), custom_call_target="tpu_custom_call", output_to_operand_aliasing={{0}: (5, {}), {1}: (6, {}), {2}: (7, {})} | custom-call | flops 1 | bytes 1048576 | tf_op jit(solution)/shard_map/attend/pallas_call | solution.py:184
  182.4 1.8 fusion.22
  184.3 3.2 collective-permute-start.14
  189.8 4.1 turn_rows.1.cot_ref
  193.9 1.9 collective-permute-start.17
  198.6 8.7 %collective-permute-done.14 = bf16[512,128]{1,0:T(8,128)(2,1)} collective-permute-done((bf16[512,128]{1,0:T(8,128)(2,1)}, bf16[512,128]{1,0:T(8,128)(2,1)}, u32[]{:S(2)}, u32[]{:S(2)}) %collective-permute-start.14) | collective-permute-done | bytes 131104 | tf_op jit(solution)/shard_map/ppermute | solution.py:643
  207.2 9.7 %collective-permute-done.15 = bf16[512,128]{1,0:T(8,128)(2,1)S(1)} collective-permute-done((bf16[512,128]{1,0:T(8,128)(2,1)}, bf16[512,128]{1,0:T(8,128)(2,1)S(1)}, u32[]{:S(2)}, u32[]{:S(2)}) %collective-permute-start.15) | collective-permute-done | bytes 131104 | tf_op jit(solution)/shard_map/ppermute | solution.py:643
  217.0 1.7 collective-permute-done.16
  218.6 2.8 collective-permute-done.17
  221.4 1.8 collective-permute-done.18
  228.5 2.1 add_convert_fusion.1
  234.7 25.7 %feed_up.1 = (f32[512,1024]{1,0:T(8,128)}, f32[512,1024]{1,0:T(8,128)}, f32[1024,2048]{1,0:T(8,128)}, bf16[4,4,4,256,128]{4,3,2,1,0:T(8,128)(2,1)}) custom-call(s32[2]{0:T(128)} %pad_add_fusion.place_ref.places_ref, bf16[512,1024]{1,0:T(8,128)(2,1)} %get-tuple-element.362.sn_ref, bf16[512,1024]{1,0:T(8,128)(2,1)} %collective-permute-done.20.got_ref, ...), custom_call_target="tpu_custom_call" | custom-call | flops 12884901888 | bytes 8388608 | tf_op jit(solution)/shard_map/feed_up/pallas_call | solution.py:448
  260.6 23.0 %feed_down.1 = (f32[512,1024]{1,0:T(8,128)}, f32[512,1024]{1,0:T(8,128)}, bf16[4,4,8,256,128]{4,3,2,1,0:T(8,128)(2,1)}, f32[4,1,512]{2,1,0:T(1,128)}) custom-call(s32[2]{0:T(128)} %pad_add_fusion.place_ref.places_ref, bf16[512,1024]{1,0:T(8,128)(2,1)} %cot_ref.1, bf16[512,1024]{1,0:T(8,128)(2,1)} %copy-done.15, bf16[512,1024]{1,0:T(8,128)(2,1)} %get-tuple-element.362.sn_ref, ...), custom_call_target="tpu_custom_call" | custom-call | flops 12884901888 | bytes 8388608 | tf_op jit(solution)/shard_map/feed_down/pallas_call | solution.py:505
  284.8 3.4 collective-permute-done.21.came_ref
  288.3 10.8 %back_norm.1 = (f32[512,1024]{1,0:T(8,128)}, bf16[8,512,128]{2,1,0:T(8,128)(2,1)}, f32[8,1024]{1,0:T(8,128)}, bf16[4,4,8,256,128]{4,3,2,1,0:T(8,128)(2,1)}) custom-call(f32[512,1024]{1,0:T(8,128)} %get-tuple-element.228.own_ref, f32[512,1024]{1,0:T(8,128)} %collective-permute-done.21.came_ref, ...), custom_call_target="tpu_custom_call", output_to_operand_aliasing={{3}: (8, {})} | custom-call | flops 2147483648 | bytes 8388608 | tf_op jit(solution)/shard_map/back_norm/pallas_call | solution.py:575
  302.1 2.4 collective-permute-start.24
  305.9 4.7 collective-permute-done.23
  310.6 2.9 collective-permute-done.24
  315.3 2.8 collective-permute-start.26
  322.0 8.6 %back_early.2 = (bf16[1024,128]{1,0:T(8,128)(2,1)}, bf16[1024,256]{1,0:T(8,128)(2,1)}, f32[1024,128]{1,0:T(8,128)}, f32[1024,128]{1,0:T(8,128)}) custom-call(s32[10]{0:T(128)} %pad_add_fusion.1.meta_ref, s32[1,2048]{1,0:T(1,128)} %bitcast.181, bf16[2048,640]{1,0:T(8,128)(2,1)} %get-tuple-element.186.q_ref.k_ref.v_ref, ...), custom_call_target="tpu_custom_call" | custom-call | flops 1 | bytes 3145728 | tf_op jit(solution)/shard_map/back_early/pallas_call | solution.py:320
  330.7 2.6 collective-permute-start.25
  336.9 9.0 %back_early.3 = (bf16[1024,128]{1,0:T(8,128)(2,1)}, bf16[1024,256]{1,0:T(8,128)(2,1)}, f32[1024,128]{1,0:T(8,128)}, f32[1024,128]{1,0:T(8,128)}) custom-call(s32[10]{0:T(128)} %pad_add_fusion.1.meta_ref, s32[1,2048]{1,0:T(1,128)} %bitcast.182, bf16[2048,640]{1,0:T(8,128)(2,1)} %get-tuple-element.186.q_ref.k_ref.v_ref, ...), custom_call_target="tpu_custom_call" | custom-call | flops 1 | bytes 3145728 | tf_op jit(solution)/shard_map/back_early/pallas_call | solution.py:320
  346.0 3.4 collective-permute-start.30
  351.0 7.2 %collective-permute-done.30.back_ref = bf16[1024,256]{1,0:T(8,128)(2,1)S(1)} collective-permute-done((bf16[1024,256]{1,0:T(8,128)(2,1)}, bf16[1024,256]{1,0:T(8,128)(2,1)S(1)}, u32[]{:S(2)}, u32[]{:S(2)}) %collective-permute-start.30) | collective-permute-done | bytes 524320 | tf_op jit(solution)/shard_map/ppermute | solution.py:654
  358.2 10.0 %back_late.2 = (bf16[2048,384]{1,0:T(8,128)(2,1)}, f32[8,128]{1,0:T(8,128)}, f32[8,384]{1,0:T(8,128)}) custom-call(s32[10]{0:T(128)} %pad_add_fusion.1.meta_ref, s32[1,2048]{1,0:T(1,128)} %bitcast.183, bf16[2048,640]{1,0:T(8,128)(2,1)} %get-tuple-element.186.q_ref.k_ref.v_ref, bf16[2048,640]{1,0:T(8,128)(2,1)} %get-tuple-element.186.q_ref.k_ref.v_ref, ...), custom_call_target="tpu_custom_call" | custom-call | flops 1 | bytes 3145728 | tf_op jit(solution)/shard_map/back_late/pallas_call | solution.py:356
  368.3 2.4 fusion.19
  370.7 1.7 collective-permute-start.31
  378.6 10.4 %back_late.3 = (bf16[2048,256]{1,0:T(8,128)(2,1)}, f32[2048,128]{1,0:T(8,128)}, f32[8,256]{1,0:T(8,128)}) custom-call(s32[10]{0:T(128)} %pad_add_fusion.1.meta_ref, s32[1,2048]{1,0:T(1,128)} %bitcast.184, bf16[2048,640]{1,0:T(8,128)(2,1)} %get-tuple-element.186.q_ref.k_ref.v_ref, bf16[2048,640]{1,0:T(8,128)(2,1)} %get-tuple-element.186.q_ref.k_ref.v_ref, ...), custom_call_target="tpu_custom_call" | custom-call | flops 1 | bytes 3145728 | tf_op jit(solution)/shard_map/back_late/pallas_call | solution.py:356
  389.6 13.3 %collective-permute-done.32.refs_4_ = bf16[512,384]{1,0:T(8,128)(2,1)} collective-permute-done((bf16[512,384]{1,0:T(8,128)(2,1)}, bf16[512,384]{1,0:T(8,128)(2,1)}, u32[]{:S(2)}, u32[]{:S(2)}) %collective-permute-start.32) | collective-permute-done | bytes 393248 | tf_op jit(solution)/shard_map/ppermute | solution.py:643
  402.9 5.5 %collective-permute-done.33.refs_6_ = bf16[512,384]{1,0:T(8,128)(2,1)} collective-permute-done((bf16[512,384]{1,0:T(8,128)(2,1)S(1)}, bf16[512,384]{1,0:T(8,128)(2,1)}, u32[]{:S(2)}, u32[]{:S(2)}) %collective-permute-start.33) | collective-permute-done | bytes 393248 | tf_op jit(solution)/shard_map/ppermute | solution.py:643
  411.5 7.1 %fusion.1 = (f32[1024]{0:T(1024)S(1)}, f32[1024]{0:T(1024)S(1)}, bf16[1024,640]{1,0:T(8,128)(2,1)S(1)}) fusion(bf16[1024,640]{1,0:T(8,128)(2,1)} %slice_dynamic-update-slice_fusion, f32[640]{0:T(1024)S(1)} %pad_maximum_fusion.11, f32[1024]{0:T(1024)} %param.22, f32[1024]{0:T(1024)} %param.23, bf16[1024,2048]{1,0:T(8,128)(2,1)} %get-tuple-element.278, ...), kind=kOutput, calls=%fused_computation.7 | convolution fusion | flops 2695493632 | bytes 9456128 | tf_op jit(solution)/shard_map/dot_general | solution.py:26
  419.7 10.5 %collective-permute-start.41 = (f32[92,128]{1,0:T(8,128)S(1)}, f32[92,128]{1,0:T(8,128)S(1)}, u32[]{:S(2)}, u32[]{:S(2)}) collective-permute-start(f32[92,128]{1,0:T(8,128)S(1)} %concatenate.78), channel_id=1, source_target_pairs={{0,4},{4,0},{8,12},{12,8},{16,20},{20,16},{24,28},{28,24},{1,5},{5... | collective-permute-start | bytes 141320 | tf_op jit(solution)/shard_map/ppermute | solution.py:648
  430.2 4.1 add_convert_fusion
  435.4 3.9 collective-permute-done.43
  442.7 2.9 collective-permute-start.35
  448.4 15.4 %collective-permute-done.46 = f32[92,128]{1,0:T(8,128)S(1)} collective-permute-done((f32[92,128]{1,0:T(8,128)S(1)}, f32[92,128]{1,0:T(8,128)S(1)}, u32[]{:S(2)}, u32[]{:S(2)}) %collective-permute-start.46) | collective-permute-done | bytes 47136 | tf_op jit(solution)/shard_map/ppermute | solution.py:648
  464.1 3.6 collective-permute-done.47
  474.7 1.7 collective-permute-start.38
  477.3 2.1 collective-permute-start.48
  479.4 4.0 collective-permute-start.49
  483.4 10.0 %front_norm.1 = f32[512,1024]{1,0:T(8,128)} custom-call(s32[2]{0:T(128)} %pad_add_fusion.place_ref.places_ref, bf16[512,384]{1,0:T(8,128)(2,1)} %get-tuple-element.277.refs_0_, bf16[512,256]{1,0:T(8,128)(2,1)} %get-tuple-element.282.refs_1_, bf16[512,384]{1,0:T(8,128)(2,1)} %collective-permute-done.31.refs_2_, ...), custom_call_target="tpu_custom_call" | custom-call | flops 2684354560 | bytes 8388608 | tf_op jit(solution)/shard_map/front_norm/pallas_call | solution.py:626
  494.6 18.6 %collective-permute-done.49 = bf16[6,256,128]{2,1,0:T(8,128)(2,1)} collective-permute-done((bf16[6,256,128]{2,1,0:T(8,128)(2,1)}, bf16[6,256,128]{2,1,0:T(8,128)(2,1)}, u32[]{:S(2)}, u32[]{:S(2)}) %collective-permute-start.49) | collective-permute-done | bytes 393248 | tf_op jit(solution)/shard_map/ppermute | solution.py:643
  513.2 3.8 collective-permute-done.50
  (279 shorter events, 86.0 us)
Async XLA Ops:
  7.2 227.4 %all-gather.5.cloned.1.call-start = ((), (), s32[]{:S(2)}) async-start(), calls=%async_computation.2 | async-start | bytes 17301504 | tf_op jit(solution)/shard_map/all_gather | solution.py:807
  12.6 24.4 %collective-permute-start = (bf16[512,1024]{1,0:T(8,128)(2,1)}, bf16[512,1024]{1,0:T(8,128)(2,1)}, u32[]{:S(2)}, u32[]{:S(2)}) collective-permute-start(bf16[512,1024]{1,0:T(8,128)(2,1)} %get-tuple-element.162.piece_ref), channel_id=1, source_target_pairs={{0,1},{1,2},{2,3},{3,0},{4,5},{5,6},{6,7},{7,4},{8,9},{9,10},{10,1... | collective-permute-start | bytes 3145736 | tf_op jit(solution)/shard_map/ppermute | solution.py:643
  19.6 42.0 %copy-start.34 = (f32[1024]{0:T(1024)S(1)}, f32[1024]{0:T(1024)}, u32[]{:S(2)}) copy-start(f32[1024]{0:T(1024)} %param.34) | copy-start | bytes 12292
  19.6 50.0 %copy-start.21 = (s32[16384]{0:T(1024)S(1)}, s32[16384]{0:T(1024)}, u32[]{:S(2)}) copy-start(s32[16384]{0:T(1024)} %param.20) | copy-start | bytes 196612
  23.9 42.7 %copy-start.4 = (bf16[512,1024]{1,0:T(8,128)(2,1)S(1)}, bf16[512,1024]{1,0:T(8,128)(2,1)}, u32[]{:S(2)}) copy-start(bf16[512,1024]{1,0:T(8,128)(2,1)} %cot_ref.1) | copy-start | bytes 3145732
  37.0 24.5 %collective-permute-start.1 = (bf16[512,1024]{1,0:T(8,128)(2,1)}, bf16[512,1024]{1,0:T(8,128)(2,1)}, u32[]{:S(2)}, u32[]{:S(2)}) collective-permute-start(bf16[512,1024]{1,0:T(8,128)(2,1)} %collective-permute-done.piece_ref), channel_id=1, source_target_pairs={{0,1},{1,2},{2,3},{3,0},{4,5},{5,6},{6,7},{7,4},{8,9},{9,10},{10,1... | collective-permute-start | bytes 3145736 | tf_op jit(solution)/shard_map/ppermute | solution.py:643
  61.5 243.0 %all-gather.7.cloned.1.call-start = ((), (), s32[]{:S(2)}) async-start(), calls=%async_computation.3 | async-start | bytes 5406720 | tf_op jit(solution)/shard_map/all_gather | solution.py:856
  61.5 18.2 %collective-permute-start.3 = (f32[1024]{0:T(1024)S(1)}, f32[1024]{0:T(1024)S(1)}, u32[]{:S(2)}, u32[]{:S(2)}) collective-permute-start(f32[1024]{0:T(1024)S(1)} %copy-done.34), channel_id=1, source_target_pairs={{0,1},{1,2},{2,3},{3,0},{4,5},{5,6},{6,7},{7,4},{8,9},{9,10},{10,1... | collective-permute-start | bytes 12296 | tf_op jit(solution)/shard_map/ppermute | solution.py:643
  61.9 17.8 %collective-permute-start.4 = (f32[1024]{0:T(1024)S(1)}, f32[1024]{0:T(1024)S(1)}, u32[]{:S(2)}, u32[]{:S(2)}) collective-permute-start(f32[1024]{0:T(1024)S(1)} %copy-done.34), channel_id=1, source_target_pairs={{0,2},{1,3},{2,0},{3,1},{4,6},{5,7},{6,4},{7,5},{8,10},{9,11},{10,... | collective-permute-start | bytes 12296 | tf_op jit(solution)/shard_map/ppermute | solution.py:643
  66.7 13.1 %collective-permute-start.5 = (f32[1024]{0:T(1024)S(1)}, f32[1024]{0:T(1024)S(1)}, u32[]{:S(2)}, u32[]{:S(2)}) collective-permute-start(f32[1024]{0:T(1024)S(1)} %copy-done.34), channel_id=1, source_target_pairs={{0,3},{1,0},{2,1},{3,2},{4,7},{5,4},{6,5},{7,6},{8,11},{9,8},{10,9... | collective-permute-start | bytes 12296 | tf_op jit(solution)/shard_map/ppermute | solution.py:643
  66.7 18.0 %collective-permute-start.6 = (bf16[512,1024]{1,0:T(8,128)(2,1)S(1)}, bf16[512,1024]{1,0:T(8,128)(2,1)S(1)}, u32[]{:S(2)}, u32[]{:S(2)}) collective-permute-start(bf16[512,1024]{1,0:T(8,128)(2,1)S(1)} %copy-done.4), channel_id=1, source_target_pairs={{0,4},{4,0},{1,5},{5,1},{2,6},{6,2},{3,7},{7,3},{8,12},{12,8},{9,1... | collective-permute-start | bytes 3145736 | tf_op jit(solution)/shard_map/ppermute | solution.py:648
  73.8 42.8 %collective-permute-start.2 = (bf16[512,1024]{1,0:T(8,128)(2,1)}, bf16[512,1024]{1,0:T(8,128)(2,1)}, u32[]{:S(2)}, u32[]{:S(2)}) collective-permute-start(bf16[512,1024]{1,0:T(8,128)(2,1)} %collective-permute-done.1.piece_ref), channel_id=1, source_target_pairs={{0,1},{1,2},{2,3},{3,0},{4,5},{5,6},{6,7},{7,4},{8,9},{9,10},{10,1... | collective-permute-start | bytes 3145736 | tf_op jit(solution)/shard_map/ppermute | solution.py:643
  84.7 36.4 %copy-start.15 = (bf16[512,1024]{1,0:T(8,128)(2,1)}, bf16[512,1024]{1,0:T(8,128)(2,1)S(1)}, u32[]{:S(2)}) copy-start(bf16[512,1024]{1,0:T(8,128)(2,1)S(1)} %collective-permute-done.6.got_ref.cot_got_ref) | copy-start | bytes 3145732
  122.3 27.8 %collective-permute-start.7 = (bf16[1024,384]{1,0:T(8,128)(2,1)S(1)}, bf16[1024,384]{1,0:T(8,128)(2,1)}, u32[]{:S(2)}, u32[]{:S(2)}) collective-permute-start(bf16[1024,384]{1,0:T(8,128)(2,1)S(1)} %slice.260), channel_id=1, source_target_pairs={{0,4},{4,8},{8,12},{12,16},{16,20},{20,24},{24,28},{1,5},{5,9},{9,... | collective-permute-start | bytes 2359304 | tf_op jit(solution)/shard_map/ppermute | solution.py:654
  126.5 23.5 %collective-permute-start.8 = (bf16[1024,128]{1,0:T(8,128)(2,1)S(1)}, bf16[1024,128]{1,0:T(8,128)(2,1)S(1)}, u32[]{:S(2)}, u32[]{:S(2)}) collective-permute-start(bf16[1024,128]{1,0:T(8,128)(2,1)S(1)} %get-tuple-element.410), channel_id=1, source_target_pairs={{0,4},{4,8},{8,12},{12,16},{16,20},{20,24},{24,28},{1,5},{5,9},{9,... | collective-permute-start | bytes 786440 | tf_op jit(solution)/shard_map/ppermute | solution.py:654
  128.5 21.6 %collective-permute-start.10 = (bf16[64,1024]{1,0:T(8,128)(2,1)S(1)}, bf16[64,1024]{1,0:T(8,128)(2,1)S(1)}, u32[]{:S(2)}, u32[]{:S(2)}) collective-permute-start(bf16[64,1024]{1,0:T(8,128)(2,1)S(1)} %constant_dynamic-slice_fusion.6), channel_id=1, source_target_pairs={{0,2},{1,3},{2,0},{3,1},{4,6},{5,7},{6,4},{7,5},{8,10},{9,11},{10,... | collective-permute-start | bytes 393224 | tf_op jit(solution)/shard_map/ppermute | solution.py:643
  131.8 18.3 %collective-permute-start.11 = (bf16[64,1024]{1,0:T(8,128)(2,1)S(1)}, bf16[64,1024]{1,0:T(8,128)(2,1)S(1)}, u32[]{:S(2)}, u32[]{:S(2)}) collective-permute-start(bf16[64,1024]{1,0:T(8,128)(2,1)S(1)} %constant_dynamic-slice_fusion.6), channel_id=1, source_target_pairs={{0,3},{1,0},{2,1},{3,2},{4,7},{5,4},{6,5},{7,6},{8,11},{9,8},{10,9... | collective-permute-start | bytes 393224 | tf_op jit(solution)/shard_map/ppermute | solution.py:643
  132.9 17.2 %collective-permute-start.9 = (bf16[64,1024]{1,0:T(8,128)(2,1)S(1)}, bf16[64,1024]{1,0:T(8,128)(2,1)S(1)}, u32[]{:S(2)}, u32[]{:S(2)}) collective-permute-start(bf16[64,1024]{1,0:T(8,128)(2,1)S(1)} %constant_dynamic-slice_fusion.6), channel_id=1, source_target_pairs={{0,1},{1,2},{2,3},{3,0},{4,5},{5,6},{6,7},{7,4},{8,9},{9,10},{10,1... | collective-permute-start | bytes 393224 | tf_op jit(solution)/shard_map/ppermute | solution.py:643
  150.2 17.6 %collective-permute-start.12 = (bf16[3,64,1024]{2,1,0:T(8,128)(2,1)S(1)}, bf16[3,64,1024]{2,1,0:T(8,128)(2,1)S(1)}, u32[]{:S(2)}, u32[]{:S(2)}) collective-permute-start(bf16[3,64,1024]{2,1,0:T(8,128)(2,1)S(1)} %pad_maximum_fusion.6), channel_id=1, source_target_pairs={{0,8},{4,12},{8,0},{12,4},{16,24},{20,28},{24,16},{28,20},{1,9},{5... | collective-permute-start | bytes 1179656 | tf_op jit(solution)/shard_map/ppermute | solution.py:648
  167.9 26.0 %collective-permute-start.19 = (bf16[3,2,64,1024]{3,2,0,1:T(8,128)(2,1)S(1)}, bf16[3,2,64,1024]{3,2,0,1:T(8,128)(2,1)}, u32[]{:S(2)}, u32[]{:S(2)}) collective-permute-start(bf16[3,2,64,1024]{3,2,0,1:T(8,128)(2,1)S(1)} %pad_maximum_fusion.3), channel_id=1, source_target_pairs={{0,4},{4,0},{1,5},{5,1},{2,6},{6,2},{3,7},{7,3},{8,12},{12,8},{9,1... | collective-permute-start | bytes 2359304 | tf_op jit(solution)/shard_map/ppermute | solution.py:648
  184.3 13.1 %collective-permute-start.13 = (bf16[512,128]{1,0:T(8,128)(2,1)}, bf16[512,128]{1,0:T(8,128)(2,1)}, u32[]{:S(2)}, u32[]{:S(2)}) collective-permute-start(bf16[512,128]{1,0:T(8,128)(2,1)} %get-tuple-element.407), channel_id=1, source_target_pairs={{0,1},{1,2},{2,3},{3,0},{4,5},{5,6},{6,7},{7,4},{8,9},{9,10},{10,1... | collective-permute-start | bytes 393224 | tf_op jit(solution)/shard_map/ppermute | solution.py:643
  184.3 22.9 %collective-permute-start.14 = (bf16[512,128]{1,0:T(8,128)(2,1)}, bf16[512,128]{1,0:T(8,128)(2,1)}, u32[]{:S(2)}, u32[]{:S(2)}) collective-permute-start(bf16[512,128]{1,0:T(8,128)(2,1)} %get-tuple-element.406), channel_id=1, source_target_pairs={{0,2},{1,3},{2,0},{3,1},{4,6},{5,7},{6,4},{7,5},{8,10},{9,11},{10,... | collective-permute-start | bytes 393224 | tf_op jit(solution)/shard_map/ppermute | solution.py:643
  187.6 29.4 %collective-permute-start.15 = (bf16[512,128]{1,0:T(8,128)(2,1)}, bf16[512,128]{1,0:T(8,128)(2,1)S(1)}, u32[]{:S(2)}, u32[]{:S(2)}) collective-permute-start(bf16[512,128]{1,0:T(8,128)(2,1)} %get-tuple-element.405), channel_id=1, source_target_pairs={{0,3},{1,0},{2,1},{3,2},{4,7},{5,4},{6,5},{7,6},{8,11},{9,8},{10,9... | collective-permute-start | bytes 393224 | tf_op jit(solution)/shard_map/ppermute | solution.py:643
  188.3 30.3 %collective-permute-start.16 = (bf16[512,128]{1,0:T(8,128)(2,1)}, bf16[512,128]{1,0:T(8,128)(2,1)}, u32[]{:S(2)}, u32[]{:S(2)}) collective-permute-start(bf16[512,128]{1,0:T(8,128)(2,1)} %get-tuple-element.403), channel_id=1, source_target_pairs={{0,1},{1,2},{2,3},{3,0},{4,5},{5,6},{6,7},{7,4},{8,9},{9,10},{10,1... | collective-permute-start | bytes 393224 | tf_op jit(solution)/shard_map/ppermute | solution.py:643
  193.9 27.5 %collective-permute-start.17 = (bf16[512,128]{1,0:T(8,128)(2,1)}, bf16[512,128]{1,0:T(8,128)(2,1)S(1)}, u32[]{:S(2)}, u32[]{:S(2)}) collective-permute-start(bf16[512,128]{1,0:T(8,128)(2,1)} %get-tuple-element.402), channel_id=1, source_target_pairs={{0,2},{1,3},{2,0},{3,1},{4,6},{5,7},{6,4},{7,5},{8,10},{9,11},{10,... | collective-permute-start | bytes 393224 | tf_op jit(solution)/shard_map/ppermute | solution.py:643
  198.2 25.1 %collective-permute-start.18 = (bf16[512,128]{1,0:T(8,128)(2,1)S(1)}, bf16[512,128]{1,0:T(8,128)(2,1)S(1)}, u32[]{:S(2)}, u32[]{:S(2)}) collective-permute-start(bf16[512,128]{1,0:T(8,128)(2,1)S(1)} %copy-done.24), channel_id=1, source_target_pairs={{0,3},{1,0},{2,1},{3,2},{4,7},{5,4},{6,5},{7,6},{8,11},{9,8},{10,9... | collective-permute-start | bytes 393224 | tf_op jit(solution)/shard_map/ppermute | solution.py:643
  198.6 29.2 %copy-start.2 = (bf16[1024,1024]{1,0:T(8,128)(2,1)}, bf16[1024,1024]{1,0:T(8,128)(2,1)S(1)}, u32[]{:S(2)}) copy-start(bf16[1024,1024]{1,0:T(8,128)(2,1)S(1)} %pad_maximum_fusion.mixing_ref) | copy-start | bytes 6291460
  198.6 27.8 %copy-start.40 = (f32[1024]{0:T(1024)S(1)}, f32[1024]{0:T(1024)}, u32[]{:S(2)}) copy-start(f32[1024]{0:T(1024)} %param.30) | copy-start | bytes 12292
  230.6 3.1 collective-permute-start.20
  234.6 144.0 %reduce-scatter.7.cloned.1.call-start = ((), (), s32[]{:S(2)}) async-start(), calls=%async_computation.4 | async-start | bytes 5242880
  260.4 211.8 %reduce-scatter.9.cloned.1.call-start = ((), (), s32[]{:S(2)}) async-start(), calls=%async_computation.5 | async-start | bytes 10485760
  283.7 4.6 collective-permute-start.21
  301.0 4.9 collective-permute-start.22
  301.0 9.6 %collective-permute-start.23 = (bf16[512,128]{1,0:T(8,128)(2,1)}, bf16[512,128]{1,0:T(8,128)(2,1)S(1)}, u32[]{:S(2)}, u32[]{:S(2)}) collective-permute-start(bf16[512,128]{1,0:T(8,128)(2,1)} %get-tuple-element.392), channel_id=1, source_target_pairs={{0,2},{1,3},{2,0},{3,1},{4,6},{5,7},{6,4},{7,5},{8,10},{9,11},{10,... | collective-permute-start | bytes 393224 | tf_op jit(solution)/shard_map/ppermute | solution.py:643
  302.1 11.4 %collective-permute-start.24 = (bf16[512,128]{1,0:T(8,128)(2,1)}, bf16[512,128]{1,0:T(8,128)(2,1)}, u32[]{:S(2)}, u32[]{:S(2)}) collective-permute-start(bf16[512,128]{1,0:T(8,128)(2,1)} %get-tuple-element.391), channel_id=1, source_target_pairs={{0,1},{1,2},{2,3},{3,0},{4,5},{5,6},{6,7},{7,4},{8,9},{9,10},{10,1... | collective-permute-start | bytes 393224 | tf_op jit(solution)/shard_map/ppermute | solution.py:643
  313.5 19.8 %collective-permute-start.29 = (f32[512,1024]{1,0:T(8,128)}, f32[512,1024]{1,0:T(8,128)}, u32[]{:S(2)}, u32[]{:S(2)}) collective-permute-start(f32[512,1024]{1,0:T(8,128)} %get-tuple-element.245), channel_id=1, source_target_pairs={{0,4},{4,0},{1,5},{5,1},{2,6},{6,2},{3,7},{7,3},{8,12},{12,8},{9,1... | collective-permute-start | bytes 6291464 | tf_op jit(solution)/shard_map/ppermute | solution.py:648
  315.3 17.9 %collective-permute-start.26 = (bf16[512,128]{1,0:T(8,128)(2,1)}, bf16[512,128]{1,0:T(8,128)(2,1)}, u32[]{:S(2)}, u32[]{:S(2)}) collective-permute-start(bf16[512,128]{1,0:T(8,128)(2,1)} %get-tuple-element.389), channel_id=1, source_target_pairs={{0,3},{1,0},{2,1},{3,2},{4,7},{5,4},{6,5},{7,6},{8,11},{9,8},{10,9... | collective-permute-start | bytes 393224 | tf_op jit(solution)/shard_map/ppermute | solution.py:643
  318.1 15.2 %collective-permute-start.27 = (bf16[512,128]{1,0:T(8,128)(2,1)}, bf16[512,128]{1,0:T(8,128)(2,1)}, u32[]{:S(2)}, u32[]{:S(2)}) collective-permute-start(bf16[512,128]{1,0:T(8,128)(2,1)} %get-tuple-element.388), channel_id=1, source_target_pairs={{0,2},{1,3},{2,0},{3,1},{4,6},{5,7},{6,4},{7,5},{8,10},{9,11},{10,... | collective-permute-start | bytes 393224 | tf_op jit(solution)/shard_map/ppermute | solution.py:643
  318.7 14.6 %collective-permute-start.28 = (bf16[512,128]{1,0:T(8,128)(2,1)}, bf16[512,128]{1,0:T(8,128)(2,1)}, u32[]{:S(2)}, u32[]{:S(2)}) collective-permute-start(bf16[512,128]{1,0:T(8,128)(2,1)} %get-tuple-element.387), channel_id=1, source_target_pairs={{0,1},{1,2},{2,3},{3,0},{4,5},{5,6},{6,7},{7,4},{8,9},{9,10},{10,1... | collective-permute-start | bytes 393224 | tf_op jit(solution)/shard_map/ppermute | solution.py:643
  330.7 20.4 %collective-permute-start.25 = (bf16[1024,256]{1,0:T(8,128)(2,1)}, bf16[1024,256]{1,0:T(8,128)(2,1)S(1)}, u32[]{:S(2)}, u32[]{:S(2)}) collective-permute-start(bf16[1024,256]{1,0:T(8,128)(2,1)} %get-tuple-element.243), channel_id=1, source_target_pairs={{4,0},{8,4},{12,8},{16,12},{20,16},{24,20},{28,24},{5,1},{9,5},{13... | collective-permute-start | bytes 1572872 | tf_op jit(solution)/shard_map/ppermute | solution.py:654
  346.0 12.2 %collective-permute-start.30 = (bf16[1024,256]{1,0:T(8,128)(2,1)}, bf16[1024,256]{1,0:T(8,128)(2,1)S(1)}, u32[]{:S(2)}, u32[]{:S(2)}) collective-permute-start(bf16[1024,256]{1,0:T(8,128)(2,1)} %get-tuple-element.255), channel_id=1, source_target_pairs={{4,0},{8,4},{12,8},{16,12},{20,16},{24,20},{28,24},{5,1},{9,5},{13... | collective-permute-start | bytes 1572872 | tf_op jit(solution)/shard_map/ppermute | solution.py:654
  370.7 18.9 %collective-permute-start.31 = (bf16[512,384]{1,0:T(8,128)(2,1)}, bf16[512,384]{1,0:T(8,128)(2,1)}, u32[]{:S(2)}, u32[]{:S(2)}) collective-permute-start(bf16[512,384]{1,0:T(8,128)(2,1)} %get-tuple-element.370), channel_id=1, source_target_pairs={{0,1},{1,2},{2,3},{3,0},{4,5},{5,6},{6,7},{7,4},{8,9},{9,10},{10,1... | collective-permute-start | bytes 1179656 | tf_op jit(solution)/shard_map/ppermute | solution.py:643
  372.5 30.5 %collective-permute-start.32 = (bf16[512,384]{1,0:T(8,128)(2,1)}, bf16[512,384]{1,0:T(8,128)(2,1)}, u32[]{:S(2)}, u32[]{:S(2)}) collective-permute-start(bf16[512,384]{1,0:T(8,128)(2,1)} %get-tuple-element.369), channel_id=1, source_target_pairs={{0,2},{1,3},{2,0},{3,1},{4,6},{5,7},{6,4},{7,5},{8,10},{9,11},{10,... | collective-permute-start | bytes 1179656 | tf_op jit(solution)/shard_map/ppermute | solution.py:643
  374.0 34.4 %collective-permute-start.33 = (bf16[512,384]{1,0:T(8,128)(2,1)S(1)}, bf16[512,384]{1,0:T(8,128)(2,1)}, u32[]{:S(2)}, u32[]{:S(2)}) collective-permute-start(bf16[512,384]{1,0:T(8,128)(2,1)S(1)} %get-tuple-element.368), channel_id=1, source_target_pairs={{0,3},{1,0},{2,1},{3,2},{4,7},{5,4},{6,5},{7,6},{8,11},{9,8},{10,9... | collective-permute-start | bytes 1179656 | tf_op jit(solution)/shard_map/ppermute | solution.py:643
  378.6 29.8 %copy-start.12 = (bf16[1,4096,128]{2,1,0:T(8,128)(2,1)S(1)}, bf16[1,4096,128]{2,1,0:T(8,128)(2,1)}, u32[]{:S(2)}) copy-start(bf16[1,4096,128]{2,1,0:T(8,128)(2,1)} %reduce-scatter.7.cloned.1.call-done) | copy-start | bytes 3145732
  409.3 10.4 %collective-permute-start.40 = (bf16[4,256,128]{2,1,0:T(8,128)(2,1)}, bf16[4,256,128]{2,1,0:T(8,128)(2,1)}, u32[]{:S(2)}, u32[]{:S(2)}) collective-permute-start(bf16[4,256,128]{2,1,0:T(8,128)(2,1)} %get-tuple-element.382), channel_id=1, source_target_pairs={{0,1},{1,2},{2,3},{3,0},{4,5},{5,6},{6,7},{7,4},{8,9},{9,10},{10,1... | collective-permute-start | bytes 786440 | tf_op jit(solution)/shard_map/ppermute | solution.py:643
  409.3 25.0 %collective-permute-start.42 = (bf16[4,256,128]{2,1,0:T(8,128)(2,1)}, bf16[4,256,128]{2,1,0:T(8,128)(2,1)}, u32[]{:S(2)}, u32[]{:S(2)}) collective-permute-start(bf16[4,256,128]{2,1,0:T(8,128)(2,1)} %get-tuple-element.381), channel_id=1, source_target_pairs={{0,2},{1,3},{2,0},{3,1},{4,6},{5,7},{6,4},{7,5},{8,10},{9,11},{10,... | collective-permute-start | bytes 786440 | tf_op jit(solution)/shard_map/ppermute | solution.py:643
  409.3 30.0 %collective-permute-start.44 = (bf16[4,256,128]{2,1,0:T(8,128)(2,1)}, bf16[4,256,128]{2,1,0:T(8,128)(2,1)}, u32[]{:S(2)}, u32[]{:S(2)}) collective-permute-start(bf16[4,256,128]{2,1,0:T(8,128)(2,1)} %get-tuple-element.380), channel_id=1, source_target_pairs={{0,3},{1,0},{2,1},{3,2},{4,7},{5,4},{6,5},{7,6},{8,11},{9,8},{10,9... | collective-permute-start | bytes 786440 | tf_op jit(solution)/shard_map/ppermute | solution.py:643
  419.7 14.6 %collective-permute-start.41 = (f32[92,128]{1,0:T(8,128)S(1)}, f32[92,128]{1,0:T(8,128)S(1)}, u32[]{:S(2)}, u32[]{:S(2)}) collective-permute-start(f32[92,128]{1,0:T(8,128)S(1)} %concatenate.78), channel_id=1, source_target_pairs={{0,4},{4,0},{8,12},{12,8},{16,20},{20,16},{24,28},{28,24},{1,5},{5... | collective-permute-start | bytes 141320 | tf_op jit(solution)/shard_map/ppermute | solution.py:648
  434.3 4.9 collective-permute-start.43
  439.3 7.8 %collective-permute-start.45 = (f32[92,128]{1,0:T(8,128)S(1)}, f32[92,128]{1,0:T(8,128)S(1)}, u32[]{:S(2)}, u32[]{:S(2)}) collective-permute-start(f32[92,128]{1,0:T(8,128)S(1)} %add.263), channel_id=1, source_target_pairs={{0,16},{4,20},{8,24},{12,28},{16,0},{20,4},{24,8},{28,12},{1,17},{... | collective-permute-start | bytes 141320 | tf_op jit(solution)/shard_map/ppermute | solution.py:648
  440.9 32.9 %collective-permute-start.37 = (bf16[2,2,128,640]{3,2,0,1:T(8,128)(2,1)S(1)}, bf16[2,2,128,640]{3,2,0,1:T(8,128)(2,1)S(1)}, u32[]{:S(2)}, u32[]{:S(2)}) collective-permute-start(bf16[2,2,128,640]{3,2,0,1:T(8,128)(2,1)S(1)} %bitcast.174), channel_id=1, source_target_pairs={{0,4},{4,0},{8,12},{12,8},{16,20},{20,16},{24,28},{28,24},{1,5},{5... | collective-permute-start | bytes 1966088 | tf_op jit(solution)/shard_map/ppermute | solution.py:648
  442.4 31.3 %collective-permute-start.34 = (bf16[512,256]{1,0:T(8,128)(2,1)}, bf16[512,256]{1,0:T(8,128)(2,1)}, u32[]{:S(2)}, u32[]{:S(2)}) collective-permute-start(bf16[512,256]{1,0:T(8,128)(2,1)} %get-tuple-element.385), channel_id=1, source_target_pairs={{0,1},{1,2},{2,3},{3,0},{4,5},{5,6},{6,7},{7,4},{8,9},{9,10},{10,1... | collective-permute-start | bytes 786440 | tf_op jit(solution)/shard_map/ppermute | solution.py:643
  442.7 31.0 %collective-permute-start.35 = (bf16[512,256]{1,0:T(8,128)(2,1)}, bf16[512,256]{1,0:T(8,128)(2,1)}, u32[]{:S(2)}, u32[]{:S(2)}) collective-permute-start(bf16[512,256]{1,0:T(8,128)(2,1)} %get-tuple-element.384), channel_id=1, source_target_pairs={{0,2},{1,3},{2,0},{3,1},{4,6},{5,7},{6,4},{7,5},{8,10},{9,11},{10,... | collective-permute-start | bytes 786440 | tf_op jit(solution)/shard_map/ppermute | solution.py:643
  445.6 28.1 %collective-permute-start.36 = (bf16[512,256]{1,0:T(8,128)(2,1)}, bf16[512,256]{1,0:T(8,128)(2,1)}, u32[]{:S(2)}, u32[]{:S(2)}) collective-permute-start(bf16[512,256]{1,0:T(8,128)(2,1)} %get-tuple-element.383), channel_id=1, source_target_pairs={{0,3},{1,0},{2,1},{3,2},{4,7},{5,4},{6,5},{7,6},{8,11},{9,8},{10,9... | collective-permute-start | bytes 786440 | tf_op jit(solution)/shard_map/ppermute | solution.py:643
  447.0 16.8 %collective-permute-start.46 = (f32[92,128]{1,0:T(8,128)S(1)}, f32[92,128]{1,0:T(8,128)S(1)}, u32[]{:S(2)}, u32[]{:S(2)}) collective-permute-start(f32[92,128]{1,0:T(8,128)S(1)} %add.264), channel_id=1, source_target_pairs={{0,1},{1,0},{2,3},{3,2},{4,5},{5,4},{6,7},{7,6},{8,9},{9,8},{10,11... | collective-permute-start | bytes 141320 | tf_op jit(solution)/shard_map/ppermute | solution.py:648
  463.8 3.9 collective-permute-start.47
  467.8 3.4 collective-permute-start.52
  474.7 18.7 %collective-permute-start.38 = (bf16[2,128,640]{2,1,0:T(8,128)(2,1)}, bf16[2,128,640]{2,1,0:T(8,128)(2,1)}, u32[]{:S(2)}, u32[]{:S(2)}) collective-permute-start(bf16[2,128,640]{2,1,0:T(8,128)(2,1)} %dynamic-slice_bitcast_fusion.2), channel_id=1, source_target_pairs={{0,8},{4,12},{8,0},{12,4},{16,24},{20,28},{24,16},{28,20},{1,9},{5... | collective-permute-start | bytes 983048 | tf_op jit(solution)/shard_map/ppermute | solution.py:648
  477.3 17.2 %collective-permute-start.48 = (bf16[6,256,128]{2,1,0:T(8,128)(2,1)}, bf16[6,256,128]{2,1,0:T(8,128)(2,1)S(1)}, u32[]{:S(2)}, u32[]{:S(2)}) collective-permute-start(bf16[6,256,128]{2,1,0:T(8,128)(2,1)} %get-tuple-element.365), channel_id=1, source_target_pairs={{0,1},{1,2},{2,3},{3,0},{4,5},{5,6},{6,7},{7,4},{8,9},{9,10},{10,1... | collective-permute-start | bytes 1179656 | tf_op jit(solution)/shard_map/ppermute | solution.py:643
  479.4 33.7 %collective-permute-start.49 = (bf16[6,256,128]{2,1,0:T(8,128)(2,1)}, bf16[6,256,128]{2,1,0:T(8,128)(2,1)}, u32[]{:S(2)}, u32[]{:S(2)}) collective-permute-start(bf16[6,256,128]{2,1,0:T(8,128)(2,1)} %get-tuple-element.367), channel_id=1, source_target_pairs={{0,2},{1,3},{2,0},{3,1},{4,6},{5,7},{6,4},{7,5},{8,10},{9,11},{10,... | collective-permute-start | bytes 1179656 | tf_op jit(solution)/shard_map/ppermute | solution.py:643
  483.4 33.6 %collective-permute-start.50 = (bf16[6,256,128]{2,1,0:T(8,128)(2,1)S(1)}, bf16[6,256,128]{2,1,0:T(8,128)(2,1)}, u32[]{:S(2)}, u32[]{:S(2)}) collective-permute-start(bf16[6,256,128]{2,1,0:T(8,128)(2,1)S(1)} %get-tuple-element.366), channel_id=1, source_target_pairs={{0,3},{1,0},{2,1},{3,2},{4,7},{5,4},{6,5},{7,6},{8,11},{9,8},{10,9... | collective-permute-start | bytes 1179656 | tf_op jit(solution)/shard_map/ppermute | solution.py:643
  494.5 25.1 %collective-permute-start.39 = (bf16[128,640]{1,0:T(8,128)(2,1)S(1)}, bf16[128,640]{1,0:T(8,128)(2,1)S(1)}, u32[]{:S(2)}, u32[]{:S(2)}) collective-permute-start(bf16[128,640]{1,0:T(8,128)(2,1)S(1)} %dynamic-slice_bitcast_fusion.6), channel_id=1, source_target_pairs={{0,16},{4,20},{8,24},{12,28},{16,0},{20,4},{24,8},{28,12},{1,17},{... | collective-permute-start | bytes 491528 | tf_op jit(solution)/shard_map/ppermute | solution.py:648
  518.4 3.3 collective-permute-start.51
  (34 other events, 161.8 us)
Sparse Core Ops, SparseCore 0:
  61.6 155.8 all-gather.4
  234.7 64.4 all-gather.6
  302.1 52.6 reduce-scatter.6
  357.7 87.7 reduce-scatter.8
where the time goes:
time: 540 us; the launch traced here: 531 us
  waiting for transfers between devices  182 us (34%)
  Pallas kernels  159 us (29%)
  starting transfers between devices  86.5 us (16%)
  local copies, waits for them, and re-layouts  50.8 us (9%)
  other arithmetic  28.2 us (5%)
  between operations  15.3 us (3%)
  matrix products  8.51 us (2%)
    ppermute x33, waiting for transfers between devices, around(): lax.ppermute(value, 'tp', [(i, (i + steps) % count) for i in range(count)])  141 us
    ppermute x33, starting transfers between devices, around(): lax.ppermute(value, 'tp', [(i, (i + steps) % count) for i in range(count)])  43.9 us
    ppermute x16, waiting for transfers between devices, flipped(): return lax.ppermute(value, axis, [(i, i ^ bit) for i in range(count)])  33.3 us
    pallas_call x4, Pallas kernels, attend(): pl.pallas_call(functools.partial(attend_kernel, base, shift), grid_spec=p...  30.3 us
    ppermute x16, starting transfers between devices, flipped(): return lax.ppermute(value, axis, [(i, i ^ bit) for i in range(count)])  30.1 us
    pallas_call x1, Pallas kernels, feed_up(): pl.pallas_call(up_kernel, grid_spec=pltpu.PrefetchScalarGridSpec(num_scal...  25.7 us
    pallas_call x1, Pallas kernels, feed_down(): pl.pallas_call(down_kernel, grid_spec=pltpu.PrefetchScalarGridSpec(num_sc...  23 us
    pallas_call x2, Pallas kernels, back_late(): pl.pallas_call(functools.partial(late_kernel, base, fresh, per, count), g...  20.4 us
  transfers between devices with their start and end apart: 57, of which 21 were waited for; matrix products, arithmetic and copies ran while one was open for 14% of the time, Pallas kernels for 30%

commit v1 on v0

--- a/solution.py
+++ b/solution.py
@@ -934,32 +934,34 @@
     output = (middle + (lost + lost_came) + down_bias).astype(BF16)
     wide_grad = nn(normed_turned, jnp.concatenate(packets, axis=1))
     weight_sum = Scatter(wide_grad.astype(BF16).reshape(seq, part, -1), seq_place)
-    pieces[1], weight_sum.parts, up_grads = tied(pieces[1], weight_sum.parts, up_grads)
+    column_sum = jnp.concatenate(column_sums)
+    columns = qkv_turned.T.astype(F32)
+    first_shift_part = jnp.sum(columns * column_sum, axis=1)
+    hat_grad = (wide_grad - first_shift[:, None] * column_sum) / first_gain[:, None]
+    first_gain_part = jnp.sum(columns * hat_grad, axis=1)
+
+    def widen(value):
+        size = value.shape[0]
+        return lax.dynamic_update_slice_in_dim(
+            jnp.zeros((size * tp,), F32), value, tp_place * size, 0
+        )
+
+    query_part = jnp.concatenate((column_sum[:PAIR], column_sum[3 * PAIR : 4 * PAIR]))
+    late_sums = (
+        first_gain_part, first_shift_part, widen(query_part),
+        widen(column_sum[2 * PAIR : 3 * PAIR]),
+    )
+    late_sums = [value.reshape(-1, PAIR) for value in late_sums]
+    sums = jnp.concatenate(late_sums + [early_sums], axis=0)
+    pieces[1], weight_sum.parts, up_grads, sums = tied(
+        pieces[1], weight_sum.parts, up_grads, sums
+    )
     up_grads = over_shards(up_grads)
     weight_sum.merge()
     stream_gradient = front_norm(
         places, [pieces[pair][k] for k in range(tp) for pair in range(2)], qkv_full, middle_back,
         first_hat, first_inverse, first_gain,
     )
-    column_sum = jnp.concatenate(column_sums)
-    columns = qkv_turned.T.astype(F32)
-    first_shift_part = jnp.sum(columns * column_sum, axis=1)
-    hat_grad = (wide_grad - first_shift[:, None] * column_sum) / first_gain[:, None]
-    first_gain_part = jnp.sum(columns * hat_grad, axis=1)
-
-    def widen(value):
-        size = value.shape[0]
-        return lax.dynamic_update_slice_in_dim(
-            jnp.zeros((size * tp,), F32), value, tp_place * size, 0
-        )
-
-    query_part = jnp.concatenate((column_sum[:PAIR], column_sum[3 * PAIR : 4 * PAIR]))
-    late_sums = (
-        first_gain_part, first_shift_part, widen(query_part),
-        widen(column_sum[2 * PAIR : 3 * PAIR]),
-    )
-    late_sums = [value.reshape(-1, PAIR) for value in late_sums]
-    sums = jnp.concatenate(late_sums + [early_sums], axis=0)
     for spot, bit in enumerate(seq_bits()):
         if spot + 1 < tp:
             sums, down_grads[spot + 1] = tied(sums, down_grads[spot + 1])

time: 540 us -> 536 us (level)
  the two profiles are of different devices: /device:TPU:13 before, /device:TPU:0 now
where the time goes in v1:
time: 536 us; the launch traced here: 526 us
  waiting for transfers between devices  169 us (32%)
  Pallas kernels  160 us (30%)
  starting transfers between devices  96.6 us (18%)
  local copies, waits for them, and re-layouts  49.3 us (9%)
  other arithmetic  27.1 us (5%)
  between operations  15.3 us (3%)
  matrix products  8.64 us (2%)
    ppermute x33, waiting for transfers between devices, around(): lax.ppermute(value, 'tp', [(i, (i + steps) % count) for i in range(count)])  123 us
    ppermute x33, starting transfers between devices, around(): lax.ppermute(value, 'tp', [(i, (i + steps) % count) for i in range(count)])  56.9 us
    ppermute x16, starting transfers between devices, flipped(): return lax.ppermute(value, axis, [(i, i ^ bit) for i in range(count)])  31.3 us
    pallas_call x4, Pallas kernels, attend(): pl.pallas_call(functools.partial(attend_kernel, base, shift), grid_spec=p...  30.7 us
    pallas_call x1, Pallas kernels, feed_up(): pl.pallas_call(up_kernel, grid_spec=pltpu.PrefetchScalarGridSpec(num_scal...  25.7 us
    unnamed x6, waiting for transfers between devices  24.9 us
    pallas_call x1, Pallas kernels, feed_down(): pl.pallas_call(down_kernel, grid_spec=pltpu.PrefetchScalarGridSpec(num_sc...  23 us
    pallas_call x2, Pallas kernels, back_late(): pl.pallas_call(functools.partial(late_kernel, base, fresh, per, count), g...  20.5 us
  transfers between devices with their start and end apart: 57, of which 19 were waited for; matrix products, arithmetic and copies ran while one was open for 13% of the time, Pallas kernels for 30%

profile of v1, /device:TPU:0, one launch (start us, length us, event | category | flops | bytes accessed | tf_op | source)
XLA Modules:
  0.0 526.1 jit_solution(8707091436774629951)
XLA Ops:
  7.3 1.5 convert_reduce_fusion.1
  8.8 1.6 fusion.8
  10.5 2.1 fusion.6
  12.6 3.1 collective-permute-start
  21.3 4.4 project.4
  25.7 15.4 %collective-permute-done.piece_ref = bf16[512,1024]{1,0:T(8,128)(2,1)} collective-permute-done((bf16[512,1024]{1,0:T(8,128)(2,1)}, bf16[512,1024]{1,0:T(8,128)(2,1)}, u32[]{:S(2)}, u32[]{:S(2)}) %collective-permute-start) | collective-permute-done | bytes 1048608 | tf_op jit(solution)/shard_map/ppermute | solution.py:643
  43.1 24.5 %collective-permute-done.1.piece_ref = bf16[512,1024]{1,0:T(8,128)(2,1)} collective-permute-done((bf16[512,1024]{1,0:T(8,128)(2,1)}, bf16[512,1024]{1,0:T(8,128)(2,1)}, u32[]{:S(2)}, u32[]{:S(2)}) %collective-permute-start.1) | collective-permute-done | bytes 1048608 | tf_op jit(solution)/shard_map/ppermute | solution.py:643
  68.0 3.6 collective-permute-start.5
  71.6 4.3 project.5
  76.4 2.5 convert_reduce_fusion
  81.3 4.3 project.6
  85.5 32.4 %collective-permute-done.2.piece_ref = bf16[512,1024]{1,0:T(8,128)(2,1)} collective-permute-done((bf16[512,1024]{1,0:T(8,128)(2,1)}, bf16[512,1024]{1,0:T(8,128)(2,1)}, u32[]{:S(2)}, u32[]{:S(2)}) %collective-permute-start.2) | collective-permute-done | bytes 1048608 | tf_op jit(solution)/shard_map/ppermute | solution.py:643
  117.9 4.4 project.7
  123.6 2.5 collective-permute-start.7
  126.1 2.9 collective-permute-start.8
  129.0 5.3 %collective-permute-start.10 = (bf16[64,1024]{1,0:T(8,128)(2,1)S(1)}, bf16[64,1024]{1,0:T(8,128)(2,1)S(1)}, u32[]{:S(2)}, u32[]{:S(2)}) collective-permute-start(bf16[64,1024]{1,0:T(8,128)(2,1)S(1)} %constant_dynamic-slice_fusion.6), channel_id=1, source_target_pairs={{0,2},{1,3},{2,0},{3,1},{4,6},{5,7},{6,4},{7,5},{8,10},{9,11},{10,... | collective-permute-start | bytes 393224 | tf_op jit(solution)/shard_map/ppermute | solution.py:643
  134.5 1.9 collective-permute-start.9
  136.3 7.8 %attend.5 = (bf16[2048,128]{1,0:T(8,128)(2,1)}, f32[128,2048]{1,0:T(8,128)}, f32[8,2048]{1,0:T(8,128)}) custom-call(s32[10]{0:T(128)} %pad_add_fusion.1.meta_ref, s32[1,2048]{1,0:T(1,128)} %bitcast.177, bf16[2048,640]{1,0:T(8,128)(2,1)} %get-tuple-element.187.q_ref.k_ref.v_ref, bf16[2048,640]{1,0:T(8,128)(2,1)} %get-tuple-element.187.q_ref.k_ref.v_ref, ...), custom_call_target="tpu_custom_call" | custom-call | flops 1 | bytes 1048576 | tf_op jit(solution)/shard_map/attend/pallas_call | solution.py:184
  144.1 8.2 %attend.4 = (bf16[2048,128]{1,0:T(8,128)(2,1)}, f32[128,2048]{1,0:T(8,128)}, f32[8,2048]{1,0:T(8,128)}) custom-call(s32[10]{0:T(128)} %pad_add_fusion.1.meta_ref, s32[1,2048]{1,0:T(1,128)} %bitcast.178, bf16[2048,640]{1,0:T(8,128)(2,1)} %get-tuple-element.187.q_ref.k_ref.v_ref, bf16[2048,640]{1,0:T(8,128)(2,1)} %get-tuple-element.187.q_ref.k_ref.v_ref, ...), custom_call_target="tpu_custom_call" | custom-call | flops 1 | bytes 1048576 | tf_op jit(solution)/shard_map/attend/pallas_call | solution.py:184
  153.6 1.6 collective-permute-start.12
  156.0 2.4 pad_maximum_fusion.1.k_ref.v_ref
  158.5 7.3 %attend.6 = (bf16[2048,128]{1,0:T(8,128)(2,1)}, f32[128,2048]{1,0:T(8,128)}, f32[8,2048]{1,0:T(8,128)}) custom-call(s32[10]{0:T(128)} %pad_add_fusion.1.meta_ref, s32[1,2048]{1,0:T(1,128)} %bitcast.179, bf16[2048,640]{1,0:T(8,128)(2,1)} %get-tuple-element.187.q_ref.k_ref.v_ref, ...), custom_call_target="tpu_custom_call", output_to_operand_aliasing={{0}: (5, {}), {1}: (6, {}), {2}: (7, {})} | custom-call | flops 1 | bytes 1048576 | tf_op jit(solution)/shard_map/attend/pallas_call | solution.py:184
  165.8 7.7 %collective-permute-done.12 = bf16[3,64,1024]{2,1,0:T(8,128)(2,1)S(1)} collective-permute-done((bf16[3,64,1024]{2,1,0:T(8,128)(2,1)S(1)}, bf16[3,64,1024]{2,1,0:T(8,128)(2,1)S(1)}, u32[]{:S(2)}, u32[]{:S(2)}) %collective-permute-start.12) | collective-permute-done | bytes 393248 | tf_op jit(solution)/shard_map/ppermute | solution.py:648
  173.6 2.7 collective-permute-start.19
  176.3 7.4 %attend.7 = (bf16[2048,128]{1,0:T(8,128)(2,1)}, f32[128,2048]{1,0:T(8,128)}, f32[8,2048]{1,0:T(8,128)}) custom-call(s32[10]{0:T(128)} %pad_add_fusion.1.meta_ref, s32[1,2048]{1,0:T(1,128)} %bitcast.180, bf16[2048,640]{1,0:T(8,128)(2,1)} %get-tuple-element.187.q_ref.k_ref.v_ref, ...), custom_call_target="tpu_custom_call", output_to_operand_aliasing={{0}: (5, {}), {1}: (6, {}), {2}: (7, {})} | custom-call | flops 1 | bytes 1048576 | tf_op jit(solution)/shard_map/attend/pallas_call | solution.py:184
  183.7 1.8 fusion.22
  186.4 2.0 collective-permute-start.14
  191.2 4.1 turn_rows.1.cot_ref
  198.5 3.1 collective-permute-start.18
  201.8 3.9 collective-permute-done.14
  205.7 8.0 %collective-permute-done.16 = bf16[512,128]{1,0:T(8,128)(2,1)} collective-permute-done((bf16[512,128]{1,0:T(8,128)(2,1)}, bf16[512,128]{1,0:T(8,128)(2,1)}, u32[]{:S(2)}, u32[]{:S(2)}) %collective-permute-start.16) | collective-permute-done | bytes 131104 | tf_op jit(solution)/shard_map/ppermute | solution.py:643
  213.7 9.2 %collective-permute-done.17 = bf16[512,128]{1,0:T(8,128)(2,1)S(1)} collective-permute-done((bf16[512,128]{1,0:T(8,128)(2,1)}, bf16[512,128]{1,0:T(8,128)(2,1)S(1)}, u32[]{:S(2)}, u32[]{:S(2)}) %collective-permute-start.17) | collective-permute-done | bytes 131104 | tf_op jit(solution)/shard_map/ppermute | solution.py:643
  228.1 2.1 add_convert_fusion.1
  234.1 25.7 %feed_up.1 = (f32[512,1024]{1,0:T(8,128)}, f32[512,1024]{1,0:T(8,128)}, f32[1024,2048]{1,0:T(8,128)}, bf16[4,4,4,256,128]{4,3,2,1,0:T(8,128)(2,1)}) custom-call(s32[2]{0:T(128)} %pad_add_fusion.place_ref.places_ref, bf16[512,1024]{1,0:T(8,128)(2,1)} %get-tuple-element.364.sn_ref, bf16[512,1024]{1,0:T(8,128)(2,1)} %collective-permute-done.20.got_ref, ...), custom_call_target="tpu_custom_call" | custom-call | flops 12884901888 | bytes 8388608 | tf_op jit(solution)/shard_map/feed_up/pallas_call | solution.py:448
  260.0 23.0 %feed_down.1 = (f32[512,1024]{1,0:T(8,128)}, f32[512,1024]{1,0:T(8,128)}, bf16[4,4,8,256,128]{4,3,2,1,0:T(8,128)(2,1)}, f32[4,1,512]{2,1,0:T(1,128)}) custom-call(s32[2]{0:T(128)} %pad_add_fusion.place_ref.places_ref, bf16[512,1024]{1,0:T(8,128)(2,1)} %cot_ref.1, bf16[512,1024]{1,0:T(8,128)(2,1)} %copy-done.15, bf16[512,1024]{1,0:T(8,128)(2,1)} %get-tuple-element.364.sn_ref, ...), custom_call_target="tpu_custom_call" | custom-call | flops 12884901888 | bytes 8388608 | tf_op jit(solution)/shard_map/feed_down/pallas_call | solution.py:505
  284.1 3.6 collective-permute-done.21.came_ref
  287.7 10.7 %back_norm.1 = (f32[512,1024]{1,0:T(8,128)}, bf16[8,512,128]{2,1,0:T(8,128)(2,1)}, f32[8,1024]{1,0:T(8,128)}, bf16[4,4,8,256,128]{4,3,2,1,0:T(8,128)(2,1)}) custom-call(f32[512,1024]{1,0:T(8,128)} %get-tuple-element.229.own_ref, f32[512,1024]{1,0:T(8,128)} %collective-permute-done.21.came_ref, ...), custom_call_target="tpu_custom_call", output_to_operand_aliasing={{3}: (8, {})} | custom-call | flops 2147483648 | bytes 8388608 | tf_op jit(solution)/shard_map/back_norm/pallas_call | solution.py:575
  300.4 4.0 collective-permute-start.22
  305.3 3.5 collective-permute-done.22
  308.7 8.7 %collective-permute-done.23 = bf16[512,128]{1,0:T(8,128)(2,1)S(1)} collective-permute-done((bf16[512,128]{1,0:T(8,128)(2,1)}, bf16[512,128]{1,0:T(8,128)(2,1)S(1)}, u32[]{:S(2)}, u32[]{:S(2)}) %collective-permute-start.23) | collective-permute-done | bytes 131104 | tf_op jit(solution)/shard_map/ppermute | solution.py:643
  319.7 2.0 collective-permute-start.28
  324.5 8.7 %back_early.2 = (bf16[1024,128]{1,0:T(8,128)(2,1)}, bf16[1024,256]{1,0:T(8,128)(2,1)}, f32[1024,128]{1,0:T(8,128)}, f32[1024,128]{1,0:T(8,128)}) custom-call(s32[10]{0:T(128)} %pad_add_fusion.1.meta_ref, s32[1,2048]{1,0:T(1,128)} %bitcast.181, bf16[2048,640]{1,0:T(8,128)(2,1)} %get-tuple-element.187.q_ref.k_ref.v_ref, ...), custom_call_target="tpu_custom_call" | custom-call | flops 1 | bytes 3145728 | tf_op jit(solution)/shard_map/back_early/pallas_call | solution.py:320
  338.1 9.2 %back_early.3 = (bf16[1024,128]{1,0:T(8,128)(2,1)}, bf16[1024,256]{1,0:T(8,128)(2,1)}, f32[1024,128]{1,0:T(8,128)}, f32[1024,128]{1,0:T(8,128)}) custom-call(s32[10]{0:T(128)} %pad_add_fusion.1.meta_ref, s32[1,2048]{1,0:T(1,128)} %bitcast.182, bf16[2048,640]{1,0:T(8,128)(2,1)} %get-tuple-element.187.q_ref.k_ref.v_ref, ...), custom_call_target="tpu_custom_call" | custom-call | flops 1 | bytes 3145728 | tf_op jit(solution)/shard_map/back_early/pallas_call | solution.py:320
  349.8 1.7 collective-permute-done.30.back_ref
  351.5 10.0 %back_late.2 = (bf16[2048,384]{1,0:T(8,128)(2,1)}, f32[8,128]{1,0:T(8,128)}, f32[8,384]{1,0:T(8,128)}) custom-call(s32[10]{0:T(128)} %pad_add_fusion.1.meta_ref, s32[1,2048]{1,0:T(1,128)} %bitcast.183, bf16[2048,640]{1,0:T(8,128)(2,1)} %get-tuple-element.187.q_ref.k_ref.v_ref, bf16[2048,640]{1,0:T(8,128)(2,1)} %get-tuple-element.187.q_ref.k_ref.v_ref, ...), custom_call_target="tpu_custom_call" | custom-call | flops 1 | bytes 3145728 | tf_op jit(solution)/shard_map/back_late/pallas_call | solution.py:356
  361.5 2.3 fusion.19
  366.5 2.8 collective-permute-start.33
  371.6 10.5 %back_late.3 = (bf16[2048,256]{1,0:T(8,128)(2,1)}, f32[2048,128]{1,0:T(8,128)}, f32[8,256]{1,0:T(8,128)}) custom-call(s32[10]{0:T(128)} %pad_add_fusion.1.meta_ref, s32[1,2048]{1,0:T(1,128)} %bitcast.184, bf16[2048,640]{1,0:T(8,128)(2,1)} %get-tuple-element.187.q_ref.k_ref.v_ref, bf16[2048,640]{1,0:T(8,128)(2,1)} %get-tuple-element.187.q_ref.k_ref.v_ref, ...), custom_call_target="tpu_custom_call" | custom-call | flops 1 | bytes 3145728 | tf_op jit(solution)/shard_map/back_late/pallas_call | solution.py:356
  382.8 11.3 %collective-permute-done.32.refs_4_ = bf16[512,384]{1,0:T(8,128)(2,1)} collective-permute-done((bf16[512,384]{1,0:T(8,128)(2,1)S(1)}, bf16[512,384]{1,0:T(8,128)(2,1)}, u32[]{:S(2)}, u32[]{:S(2)}) %collective-permute-start.32) | collective-permute-done | bytes 393248 | tf_op jit(solution)/shard_map/ppermute | solution.py:643
  394.1 7.3 %fusion.1 = (f32[1024]{0:T(1024)S(1)}, f32[1024]{0:T(1024)S(1)}, bf16[1024,640]{1,0:T(8,128)(2,1)S(1)}) fusion(bf16[1024,640]{1,0:T(8,128)(2,1)} %slice_dynamic-update-slice_fusion, f32[640]{0:T(1024)S(1)} %pad_maximum_fusion.11, f32[1024]{0:T(1024)S(1)} %copy-done.29, f32[1024]{0:T(1024)S(1)} %copy-done.33, bf16[1024,2048]{1,0:T(8,128)(2,1)} %get-tuple-element.279, ...), kind=kOutput, calls=%fused_computation.7 | convolution fusion | flops 2695493632 | bytes 9456128 | tf_op jit(solution)/shard_map/dot_general | solution.py:26
  404.1 8.5 %collective-permute-start.34 = (bf16[512,256]{1,0:T(8,128)(2,1)}, bf16[512,256]{1,0:T(8,128)(2,1)}, u32[]{:S(2)}, u32[]{:S(2)}) collective-permute-start(bf16[512,256]{1,0:T(8,128)(2,1)} %get-tuple-element.387), channel_id=1, source_target_pairs={{0,1},{1,2},{2,3},{3,0},{4,5},{5,6},{6,7},{7,4},{8,9},{9,10},{10,1... | collective-permute-start | bytes 786440 | tf_op jit(solution)/shard_map/ppermute | solution.py:643
  417.7 4.0 add_convert_fusion
  421.6 24.8 %reduce-scatter.9.cloned.1.call-done = bf16[1,8192,128]{2,1,0:T(8,128)(2,1)} async-done(((bf16[4,8192,128]{2,1,0:T(8,128)(2,1)}), bf16[1,8192,128]{2,1,0:T(8,128)(2,1)}) %reduce-scatter.9.cloned.1.call-update) | async-done | bytes 2097168
  446.5 1.6 slice.330
  448.0 2.5 collective-permute-start.42
  455.9 3.0 collective-permute-start.50
  458.8 6.0 %collective-permute-done.42 = bf16[4,256,128]{2,1,0:T(8,128)(2,1)S(1)} collective-permute-done((bf16[4,256,128]{2,1,0:T(8,128)(2,1)S(1)}, bf16[4,256,128]{2,1,0:T(8,128)(2,1)S(1)}, u32[]{:S(2)}, u32[]{:S(2)}) %collective-permute-start.42) | collective-permute-done | bytes 262176 | tf_op jit(solution)/shard_map/ppermute | solution.py:643
  466.3 3.1 collective-permute-done.43
  471.7 10.0 %front_norm.1 = f32[512,1024]{1,0:T(8,128)} custom-call(s32[2]{0:T(128)} %pad_add_fusion.place_ref.places_ref, bf16[512,384]{1,0:T(8,128)(2,1)} %get-tuple-element.278.refs_0_, bf16[512,256]{1,0:T(8,128)(2,1)} %get-tuple-element.287.refs_1_, bf16[512,384]{1,0:T(8,128)(2,1)} %collective-permute-done.31.refs_2_, ...), custom_call_target="tpu_custom_call" | custom-call | flops 2684354560 | bytes 8388608 | tf_op jit(solution)/shard_map/front_norm/pallas_call | solution.py:626
  481.7 17.2 %collective-permute-start.46 = (f32[92,128]{1,0:T(8,128)S(1)}, f32[92,128]{1,0:T(8,128)S(1)}, u32[]{:S(2)}, u32[]{:S(2)}) collective-permute-start(f32[92,128]{1,0:T(8,128)S(1)} %add.264), channel_id=1, source_target_pairs={{0,1},{1,0},{2,3},{3,2},{4,5},{5,4},{6,7},{7,6},{8,9},{9,8},{10,11... | collective-permute-start | bytes 141320 | tf_op jit(solution)/shard_map/ppermute | solution.py:648
  501.0 3.3 collective-permute-start.47
  504.3 2.0 collective-permute-done.47
  508.3 1.5 collective-permute-start.39
  512.8 2.2 collective-permute-done.39
  (277 shorter events, 80.3 us)
Async XLA Ops:
  7.2 226.8 %all-gather.5.cloned.1.call-start = ((), (), s32[]{:S(2)}) async-start(), calls=%async_computation.2 | async-start | bytes 17301504 | tf_op jit(solution)/shard_map/all_gather | solution.py:807
  12.6 28.5 %collective-permute-start = (bf16[512,1024]{1,0:T(8,128)(2,1)}, bf16[512,1024]{1,0:T(8,128)(2,1)}, u32[]{:S(2)}, u32[]{:S(2)}) collective-permute-start(bf16[512,1024]{1,0:T(8,128)(2,1)} %get-tuple-element.163.piece_ref), channel_id=1, source_target_pairs={{0,1},{1,2},{2,3},{3,0},{4,5},{5,6},{6,7},{7,4},{8,9},{9,10},{10,1... | collective-permute-start | bytes 3145736 | tf_op jit(solution)/shard_map/ppermute | solution.py:643
  21.3 46.4 %copy-start.35 = (f32[1024]{0:T(1024)S(1)}, f32[1024]{0:T(1024)}, u32[]{:S(2)}) copy-start(f32[1024]{0:T(1024)} %param.34) | copy-start | bytes 12292
  21.3 50.3 %copy-start.21 = (s32[16384]{0:T(1024)S(1)}, s32[16384]{0:T(1024)}, u32[]{:S(2)}) copy-start(s32[16384]{0:T(1024)} %param.20) | copy-start | bytes 196612
  25.7 45.8 %copy-start.4 = (bf16[512,1024]{1,0:T(8,128)(2,1)S(1)}, bf16[512,1024]{1,0:T(8,128)(2,1)}, u32[]{:S(2)}) copy-start(bf16[512,1024]{1,0:T(8,128)(2,1)} %cot_ref.1) | copy-start | bytes 3145732
  41.2 26.4 %collective-permute-start.1 = (bf16[512,1024]{1,0:T(8,128)(2,1)}, bf16[512,1024]{1,0:T(8,128)(2,1)}, u32[]{:S(2)}, u32[]{:S(2)}) collective-permute-start(bf16[512,1024]{1,0:T(8,128)(2,1)} %collective-permute-done.piece_ref), channel_id=1, source_target_pairs={{0,1},{1,2},{2,3},{3,0},{4,5},{5,6},{6,7},{7,4},{8,9},{9,10},{10,1... | collective-permute-start | bytes 3145736 | tf_op jit(solution)/shard_map/ppermute | solution.py:643
  67.6 237.6 %all-gather.7.cloned.1.call-start = ((), (), s32[]{:S(2)}) async-start(), calls=%async_computation.3 | async-start | bytes 5406720 | tf_op jit(solution)/shard_map/all_gather | solution.py:856
  67.7 12.9 %collective-permute-start.3 = (f32[1024]{0:T(1024)S(1)}, f32[1024]{0:T(1024)S(1)}, u32[]{:S(2)}, u32[]{:S(2)}) collective-permute-start(f32[1024]{0:T(1024)S(1)} %copy-done.35), channel_id=1, source_target_pairs={{0,1},{1,2},{2,3},{3,0},{4,5},{5,6},{6,7},{7,4},{8,9},{9,10},{10,1... | collective-permute-start | bytes 12296 | tf_op jit(solution)/shard_map/ppermute | solution.py:643
  67.8 12.8 %collective-permute-start.4 = (f32[1024]{0:T(1024)S(1)}, f32[1024]{0:T(1024)S(1)}, u32[]{:S(2)}, u32[]{:S(2)}) collective-permute-start(f32[1024]{0:T(1024)S(1)} %copy-done.35), channel_id=1, source_target_pairs={{0,2},{1,3},{2,0},{3,1},{4,6},{5,7},{6,4},{7,5},{8,10},{9,11},{10,... | collective-permute-start | bytes 12296 | tf_op jit(solution)/shard_map/ppermute | solution.py:643
  68.0 12.6 %collective-permute-start.5 = (f32[1024]{0:T(1024)S(1)}, f32[1024]{0:T(1024)S(1)}, u32[]{:S(2)}, u32[]{:S(2)}) collective-permute-start(f32[1024]{0:T(1024)S(1)} %copy-done.35), channel_id=1, source_target_pairs={{0,3},{1,0},{2,1},{3,2},{4,7},{5,4},{6,5},{7,6},{8,11},{9,8},{10,9... | collective-permute-start | bytes 12296 | tf_op jit(solution)/shard_map/ppermute | solution.py:643
  71.6 14.0 %collective-permute-start.6 = (bf16[512,1024]{1,0:T(8,128)(2,1)S(1)}, bf16[512,1024]{1,0:T(8,128)(2,1)S(1)}, u32[]{:S(2)}, u32[]{:S(2)}) collective-permute-start(bf16[512,1024]{1,0:T(8,128)(2,1)S(1)} %copy-done.4), channel_id=1, source_target_pairs={{0,4},{4,0},{1,5},{5,1},{2,6},{6,2},{3,7},{7,3},{8,12},{12,8},{9,1... | collective-permute-start | bytes 3145736 | tf_op jit(solution)/shard_map/ppermute | solution.py:648
  76.0 42.0 %collective-permute-start.2 = (bf16[512,1024]{1,0:T(8,128)(2,1)}, bf16[512,1024]{1,0:T(8,128)(2,1)}, u32[]{:S(2)}, u32[]{:S(2)}) collective-permute-start(bf16[512,1024]{1,0:T(8,128)(2,1)} %collective-permute-done.1.piece_ref), channel_id=1, source_target_pairs={{0,1},{1,2},{2,3},{3,0},{4,5},{5,6},{6,7},{7,4},{8,9},{9,10},{10,1... | collective-permute-start | bytes 3145736 | tf_op jit(solution)/shard_map/ppermute | solution.py:643
  85.5 36.8 %copy-start.15 = (bf16[512,1024]{1,0:T(8,128)(2,1)}, bf16[512,1024]{1,0:T(8,128)(2,1)S(1)}, u32[]{:S(2)}) copy-start(bf16[512,1024]{1,0:T(8,128)(2,1)S(1)} %collective-permute-done.6.got_ref.cot_got_ref) | copy-start | bytes 3145732
  123.6 30.0 %collective-permute-start.7 = (bf16[1024,384]{1,0:T(8,128)(2,1)S(1)}, bf16[1024,384]{1,0:T(8,128)(2,1)}, u32[]{:S(2)}, u32[]{:S(2)}) collective-permute-start(bf16[1024,384]{1,0:T(8,128)(2,1)S(1)} %slice.260), channel_id=1, source_target_pairs={{0,4},{4,8},{8,12},{12,16},{16,20},{20,24},{24,28},{1,5},{5,9},{9,... | collective-permute-start | bytes 2359304 | tf_op jit(solution)/shard_map/ppermute | solution.py:654
  126.1 27.4 %collective-permute-start.8 = (bf16[1024,128]{1,0:T(8,128)(2,1)S(1)}, bf16[1024,128]{1,0:T(8,128)(2,1)S(1)}, u32[]{:S(2)}, u32[]{:S(2)}) collective-permute-start(bf16[1024,128]{1,0:T(8,128)(2,1)S(1)} %get-tuple-element.412), channel_id=1, source_target_pairs={{0,4},{4,8},{8,12},{12,16},{16,20},{20,24},{24,28},{1,5},{5,9},{9,... | collective-permute-start | bytes 786440 | tf_op jit(solution)/shard_map/ppermute | solution.py:654
  129.0 24.5 %collective-permute-start.10 = (bf16[64,1024]{1,0:T(8,128)(2,1)S(1)}, bf16[64,1024]{1,0:T(8,128)(2,1)S(1)}, u32[]{:S(2)}, u32[]{:S(2)}) collective-permute-start(bf16[64,1024]{1,0:T(8,128)(2,1)S(1)} %constant_dynamic-slice_fusion.6), channel_id=1, source_target_pairs={{0,2},{1,3},{2,0},{3,1},{4,6},{5,7},{6,4},{7,5},{8,10},{9,11},{10,... | collective-permute-start | bytes 393224 | tf_op jit(solution)/shard_map/ppermute | solution.py:643
  134.3 19.2 %collective-permute-start.11 = (bf16[64,1024]{1,0:T(8,128)(2,1)S(1)}, bf16[64,1024]{1,0:T(8,128)(2,1)S(1)}, u32[]{:S(2)}, u32[]{:S(2)}) collective-permute-start(bf16[64,1024]{1,0:T(8,128)(2,1)S(1)} %constant_dynamic-slice_fusion.6), channel_id=1, source_target_pairs={{0,3},{1,0},{2,1},{3,2},{4,7},{5,4},{6,5},{7,6},{8,11},{9,8},{10,9... | collective-permute-start | bytes 393224 | tf_op jit(solution)/shard_map/ppermute | solution.py:643
  134.5 19.1 %collective-permute-start.9 = (bf16[64,1024]{1,0:T(8,128)(2,1)S(1)}, bf16[64,1024]{1,0:T(8,128)(2,1)S(1)}, u32[]{:S(2)}, u32[]{:S(2)}) collective-permute-start(bf16[64,1024]{1,0:T(8,128)(2,1)S(1)} %constant_dynamic-slice_fusion.6), channel_id=1, source_target_pairs={{0,1},{1,2},{2,3},{3,0},{4,5},{5,6},{6,7},{7,4},{8,9},{9,10},{10,1... | collective-permute-start | bytes 393224 | tf_op jit(solution)/shard_map/ppermute | solution.py:643
  153.6 19.8 %collective-permute-start.12 = (bf16[3,64,1024]{2,1,0:T(8,128)(2,1)S(1)}, bf16[3,64,1024]{2,1,0:T(8,128)(2,1)S(1)}, u32[]{:S(2)}, u32[]{:S(2)}) collective-permute-start(bf16[3,64,1024]{2,1,0:T(8,128)(2,1)S(1)} %pad_maximum_fusion.6), channel_id=1, source_target_pairs={{0,8},{4,12},{8,0},{12,4},{16,24},{20,28},{24,16},{28,20},{1,9},{5... | collective-permute-start | bytes 1179656 | tf_op jit(solution)/shard_map/ppermute | solution.py:648
  173.6 21.7 %collective-permute-start.19 = (bf16[3,2,64,1024]{3,2,0,1:T(8,128)(2,1)S(1)}, bf16[3,2,64,1024]{3,2,0,1:T(8,128)(2,1)}, u32[]{:S(2)}, u32[]{:S(2)}) collective-permute-start(bf16[3,2,64,1024]{3,2,0,1:T(8,128)(2,1)S(1)} %pad_maximum_fusion.3), channel_id=1, source_target_pairs={{0,4},{4,0},{1,5},{5,1},{2,6},{6,2},{3,7},{7,3},{8,12},{12,8},{9,1... | collective-permute-start | bytes 2359304 | tf_op jit(solution)/shard_map/ppermute | solution.py:648
  185.5 12.3 %collective-permute-start.13 = (bf16[512,128]{1,0:T(8,128)(2,1)}, bf16[512,128]{1,0:T(8,128)(2,1)}, u32[]{:S(2)}, u32[]{:S(2)}) collective-permute-start(bf16[512,128]{1,0:T(8,128)(2,1)} %get-tuple-element.409), channel_id=1, source_target_pairs={{0,1},{1,2},{2,3},{3,0},{4,5},{5,6},{6,7},{7,4},{8,9},{9,10},{10,1... | collective-permute-start | bytes 393224 | tf_op jit(solution)/shard_map/ppermute | solution.py:643
  186.4 19.3 %collective-permute-start.14 = (bf16[512,128]{1,0:T(8,128)(2,1)}, bf16[512,128]{1,0:T(8,128)(2,1)}, u32[]{:S(2)}, u32[]{:S(2)}) collective-permute-start(bf16[512,128]{1,0:T(8,128)(2,1)} %get-tuple-element.408), channel_id=1, source_target_pairs={{0,2},{1,3},{2,0},{3,1},{4,6},{5,7},{6,4},{7,5},{8,10},{9,11},{10,... | collective-permute-start | bytes 393224 | tf_op jit(solution)/shard_map/ppermute | solution.py:643
  188.4 17.3 %collective-permute-start.15 = (bf16[512,128]{1,0:T(8,128)(2,1)}, bf16[512,128]{1,0:T(8,128)(2,1)S(1)}, u32[]{:S(2)}, u32[]{:S(2)}) collective-permute-start(bf16[512,128]{1,0:T(8,128)(2,1)} %get-tuple-element.407), channel_id=1, source_target_pairs={{0,3},{1,0},{2,1},{3,2},{4,7},{5,4},{6,5},{7,6},{8,11},{9,8},{10,9... | collective-permute-start | bytes 393224 | tf_op jit(solution)/shard_map/ppermute | solution.py:643
  190.1 23.6 %collective-permute-start.16 = (bf16[512,128]{1,0:T(8,128)(2,1)}, bf16[512,128]{1,0:T(8,128)(2,1)}, u32[]{:S(2)}, u32[]{:S(2)}) collective-permute-start(bf16[512,128]{1,0:T(8,128)(2,1)} %get-tuple-element.405), channel_id=1, source_target_pairs={{0,1},{1,2},{2,3},{3,0},{4,5},{5,6},{6,7},{7,4},{8,9},{9,10},{10,1... | collective-permute-start | bytes 393224 | tf_op jit(solution)/shard_map/ppermute | solution.py:643
  195.3 27.6 %collective-permute-start.17 = (bf16[512,128]{1,0:T(8,128)(2,1)}, bf16[512,128]{1,0:T(8,128)(2,1)S(1)}, u32[]{:S(2)}, u32[]{:S(2)}) collective-permute-start(bf16[512,128]{1,0:T(8,128)(2,1)} %get-tuple-element.404), channel_id=1, source_target_pairs={{0,2},{1,3},{2,0},{3,1},{4,6},{5,7},{6,4},{7,5},{8,10},{9,11},{10,... | collective-permute-start | bytes 393224 | tf_op jit(solution)/shard_map/ppermute | solution.py:643
  198.5 24.3 %collective-permute-start.18 = (bf16[512,128]{1,0:T(8,128)(2,1)S(1)}, bf16[512,128]{1,0:T(8,128)(2,1)S(1)}, u32[]{:S(2)}, u32[]{:S(2)}) collective-permute-start(bf16[512,128]{1,0:T(8,128)(2,1)S(1)} %copy-done.28), channel_id=1, source_target_pairs={{0,3},{1,0},{2,1},{3,2},{4,7},{5,4},{6,5},{7,6},{8,11},{9,8},{10,9... | collective-permute-start | bytes 393224 | tf_op jit(solution)/shard_map/ppermute | solution.py:643
  201.8 25.5 %copy-start.2 = (bf16[1024,1024]{1,0:T(8,128)(2,1)}, bf16[1024,1024]{1,0:T(8,128)(2,1)S(1)}, u32[]{:S(2)}) copy-start(bf16[1024,1024]{1,0:T(8,128)(2,1)S(1)} %pad_maximum_fusion.mixing_ref) | copy-start | bytes 6291460
  201.8 24.1 %copy-start.39 = (f32[1024]{0:T(1024)S(1)}, f32[1024]{0:T(1024)}, u32[]{:S(2)}) copy-start(f32[1024]{0:T(1024)} %param.30) | copy-start | bytes 12292
  230.2 3.0 collective-permute-start.20
  234.0 137.6 %reduce-scatter.7.cloned.1.call-start = ((), (), s32[]{:S(2)}) async-start(), calls=%async_computation.4 | async-start | bytes 5242880
  259.8 186.7 %reduce-scatter.9.cloned.1.call-start = ((), (), s32[]{:S(2)}) async-start(), calls=%async_computation.5 | async-start | bytes 10485760
  283.0 4.7 collective-permute-start.21
  300.4 8.3 %collective-permute-start.22 = (bf16[512,128]{1,0:T(8,128)(2,1)}, bf16[512,128]{1,0:T(8,128)(2,1)S(1)}, u32[]{:S(2)}, u32[]{:S(2)}) collective-permute-start(bf16[512,128]{1,0:T(8,128)(2,1)} %get-tuple-element.395), channel_id=1, source_target_pairs={{0,3},{1,0},{2,1},{3,2},{4,7},{5,4},{6,5},{7,6},{8,11},{9,8},{10,9... | collective-permute-start | bytes 393224 | tf_op jit(solution)/shard_map/ppermute | solution.py:643
  304.4 13.0 %collective-permute-start.23 = (bf16[512,128]{1,0:T(8,128)(2,1)}, bf16[512,128]{1,0:T(8,128)(2,1)S(1)}, u32[]{:S(2)}, u32[]{:S(2)}) collective-permute-start(bf16[512,128]{1,0:T(8,128)(2,1)} %get-tuple-element.394), channel_id=1, source_target_pairs={{0,2},{1,3},{2,0},{3,1},{4,6},{5,7},{6,4},{7,5},{8,10},{9,11},{10,... | collective-permute-start | bytes 393224 | tf_op jit(solution)/shard_map/ppermute | solution.py:643
  305.2 12.2 %collective-permute-start.24 = (bf16[512,128]{1,0:T(8,128)(2,1)}, bf16[512,128]{1,0:T(8,128)(2,1)}, u32[]{:S(2)}, u32[]{:S(2)}) collective-permute-start(bf16[512,128]{1,0:T(8,128)(2,1)} %get-tuple-element.393), channel_id=1, source_target_pairs={{0,1},{1,2},{2,3},{3,0},{4,5},{5,6},{6,7},{7,4},{8,9},{9,10},{10,1... | collective-permute-start | bytes 393224 | tf_op jit(solution)/shard_map/ppermute | solution.py:643
  318.1 16.4 %collective-permute-start.29 = (f32[512,1024]{1,0:T(8,128)}, f32[512,1024]{1,0:T(8,128)}, u32[]{:S(2)}, u32[]{:S(2)}) collective-permute-start(f32[512,1024]{1,0:T(8,128)} %get-tuple-element.246), channel_id=1, source_target_pairs={{0,4},{4,0},{1,5},{5,1},{2,6},{6,2},{3,7},{7,3},{8,12},{12,8},{9,1... | collective-permute-start | bytes 6291464 | tf_op jit(solution)/shard_map/ppermute | solution.py:648
  318.8 15.6 %collective-permute-start.26 = (bf16[512,128]{1,0:T(8,128)(2,1)}, bf16[512,128]{1,0:T(8,128)(2,1)}, u32[]{:S(2)}, u32[]{:S(2)}) collective-permute-start(bf16[512,128]{1,0:T(8,128)(2,1)} %get-tuple-element.391), channel_id=1, source_target_pairs={{0,3},{1,0},{2,1},{3,2},{4,7},{5,4},{6,5},{7,6},{8,11},{9,8},{10,9... | collective-permute-start | bytes 393224 | tf_op jit(solution)/shard_map/ppermute | solution.py:643
  319.0 15.5 %collective-permute-start.27 = (bf16[512,128]{1,0:T(8,128)(2,1)}, bf16[512,128]{1,0:T(8,128)(2,1)}, u32[]{:S(2)}, u32[]{:S(2)}) collective-permute-start(bf16[512,128]{1,0:T(8,128)(2,1)} %get-tuple-element.390), channel_id=1, source_target_pairs={{0,2},{1,3},{2,0},{3,1},{4,6},{5,7},{6,4},{7,5},{8,10},{9,11},{10,... | collective-permute-start | bytes 393224 | tf_op jit(solution)/shard_map/ppermute | solution.py:643
  319.7 14.8 %collective-permute-start.28 = (bf16[512,128]{1,0:T(8,128)(2,1)}, bf16[512,128]{1,0:T(8,128)(2,1)}, u32[]{:S(2)}, u32[]{:S(2)}) collective-permute-start(bf16[512,128]{1,0:T(8,128)(2,1)} %get-tuple-element.389), channel_id=1, source_target_pairs={{0,1},{1,2},{2,3},{3,0},{4,5},{5,6},{6,7},{7,4},{8,9},{9,10},{10,1... | collective-permute-start | bytes 393224 | tf_op jit(solution)/shard_map/ppermute | solution.py:643
  333.2 16.6 %collective-permute-start.25 = (bf16[1024,256]{1,0:T(8,128)(2,1)}, bf16[1024,256]{1,0:T(8,128)(2,1)S(1)}, u32[]{:S(2)}, u32[]{:S(2)}) collective-permute-start(bf16[1024,256]{1,0:T(8,128)(2,1)} %get-tuple-element.244), channel_id=1, source_target_pairs={{4,0},{8,4},{12,8},{16,12},{20,16},{24,20},{28,24},{5,1},{9,5},{13... | collective-permute-start | bytes 1572872 | tf_op jit(solution)/shard_map/ppermute | solution.py:654
  347.3 4.2 collective-permute-start.30
  363.8 19.0 %collective-permute-start.31 = (bf16[512,384]{1,0:T(8,128)(2,1)S(1)}, bf16[512,384]{1,0:T(8,128)(2,1)}, u32[]{:S(2)}, u32[]{:S(2)}) collective-permute-start(bf16[512,384]{1,0:T(8,128)(2,1)S(1)} %get-tuple-element.372), channel_id=1, source_target_pairs={{0,1},{1,2},{2,3},{3,0},{4,5},{5,6},{6,7},{7,4},{8,9},{9,10},{10,1... | collective-permute-start | bytes 1179656 | tf_op jit(solution)/shard_map/ppermute | solution.py:643
  365.0 29.0 %collective-permute-start.32 = (bf16[512,384]{1,0:T(8,128)(2,1)S(1)}, bf16[512,384]{1,0:T(8,128)(2,1)}, u32[]{:S(2)}, u32[]{:S(2)}) collective-permute-start(bf16[512,384]{1,0:T(8,128)(2,1)S(1)} %get-tuple-element.371), channel_id=1, source_target_pairs={{0,2},{1,3},{2,0},{3,1},{4,6},{5,7},{6,4},{7,5},{8,10},{9,11},{10,... | collective-permute-start | bytes 1179656 | tf_op jit(solution)/shard_map/ppermute | solution.py:643
  366.5 27.6 %collective-permute-start.33 = (bf16[512,384]{1,0:T(8,128)(2,1)S(1)}, bf16[512,384]{1,0:T(8,128)(2,1)}, u32[]{:S(2)}, u32[]{:S(2)}) collective-permute-start(bf16[512,384]{1,0:T(8,128)(2,1)S(1)} %get-tuple-element.370), channel_id=1, source_target_pairs={{0,3},{1,0},{2,1},{3,2},{4,7},{5,4},{6,5},{7,6},{8,11},{9,8},{10,9... | collective-permute-start | bytes 1179656 | tf_op jit(solution)/shard_map/ppermute | solution.py:643
  401.5 50.4 %collective-permute-start.37 = (bf16[2,2,128,640]{3,2,0,1:T(8,128)(2,1)S(1)}, bf16[2,2,128,640]{3,2,0,1:T(8,128)(2,1)}, u32[]{:S(2)}, u32[]{:S(2)}) collective-permute-start(bf16[2,2,128,640]{3,2,0,1:T(8,128)(2,1)S(1)} %bitcast.174), channel_id=1, source_target_pairs={{0,4},{4,0},{8,12},{12,8},{16,20},{20,16},{24,28},{28,24},{1,5},{5... | collective-permute-start | bytes 1966088 | tf_op jit(solution)/shard_map/ppermute | solution.py:648
  404.1 43.9 %collective-permute-start.34 = (bf16[512,256]{1,0:T(8,128)(2,1)}, bf16[512,256]{1,0:T(8,128)(2,1)}, u32[]{:S(2)}, u32[]{:S(2)}) collective-permute-start(bf16[512,256]{1,0:T(8,128)(2,1)} %get-tuple-element.387), channel_id=1, source_target_pairs={{0,1},{1,2},{2,3},{3,0},{4,5},{5,6},{6,7},{7,4},{8,9},{9,10},{10,1... | collective-permute-start | bytes 786440 | tf_op jit(solution)/shard_map/ppermute | solution.py:643
  412.6 37.9 %collective-permute-start.35 = (bf16[512,256]{1,0:T(8,128)(2,1)}, bf16[512,256]{1,0:T(8,128)(2,1)}, u32[]{:S(2)}, u32[]{:S(2)}) collective-permute-start(bf16[512,256]{1,0:T(8,128)(2,1)} %get-tuple-element.386), channel_id=1, source_target_pairs={{0,2},{1,3},{2,0},{3,1},{4,6},{5,7},{6,4},{7,5},{8,10},{9,11},{10,... | collective-permute-start | bytes 786440 | tf_op jit(solution)/shard_map/ppermute | solution.py:643
  413.7 38.3 %collective-permute-start.36 = (bf16[512,256]{1,0:T(8,128)(2,1)}, bf16[512,256]{1,0:T(8,128)(2,1)}, u32[]{:S(2)}, u32[]{:S(2)}) collective-permute-start(bf16[512,256]{1,0:T(8,128)(2,1)} %get-tuple-element.385), channel_id=1, source_target_pairs={{0,3},{1,0},{2,1},{3,2},{4,7},{5,4},{6,5},{7,6},{8,11},{9,8},{10,9... | collective-permute-start | bytes 786440 | tf_op jit(solution)/shard_map/ppermute | solution.py:643
  415.8 36.1 %collective-permute-start.40 = (bf16[4,256,128]{2,1,0:T(8,128)(2,1)}, bf16[4,256,128]{2,1,0:T(8,128)(2,1)}, u32[]{:S(2)}, u32[]{:S(2)}) collective-permute-start(bf16[4,256,128]{2,1,0:T(8,128)(2,1)} %get-tuple-element.384), channel_id=1, source_target_pairs={{0,1},{1,2},{2,3},{3,0},{4,5},{5,6},{6,7},{7,4},{8,9},{9,10},{10,1... | collective-permute-start | bytes 786440 | tf_op jit(solution)/shard_map/ppermute | solution.py:643
  421.6 28.9 %copy-start.22 = (bf16[4,256,128]{2,1,0:T(8,128)(2,1)S(1)}, bf16[4,256,128]{2,1,0:T(8,128)(2,1)}, u32[]{:S(2)}) copy-start(bf16[4,256,128]{2,1,0:T(8,128)(2,1)} %get-tuple-element.382) | copy-start | bytes 786436
  448.0 16.8 %collective-permute-start.42 = (bf16[4,256,128]{2,1,0:T(8,128)(2,1)S(1)}, bf16[4,256,128]{2,1,0:T(8,128)(2,1)S(1)}, u32[]{:S(2)}, u32[]{:S(2)}) collective-permute-start(bf16[4,256,128]{2,1,0:T(8,128)(2,1)S(1)} %copy-done.25), channel_id=1, source_target_pairs={{0,2},{1,3},{2,0},{3,1},{4,6},{5,7},{6,4},{7,5},{8,10},{9,11},{10,... | collective-permute-start | bytes 786440 | tf_op jit(solution)/shard_map/ppermute | solution.py:643
  450.5 20.4 %collective-permute-start.44 = (bf16[4,256,128]{2,1,0:T(8,128)(2,1)S(1)}, bf16[4,256,128]{2,1,0:T(8,128)(2,1)S(1)}, u32[]{:S(2)}, u32[]{:S(2)}) collective-permute-start(bf16[4,256,128]{2,1,0:T(8,128)(2,1)S(1)} %copy-done.22), channel_id=1, source_target_pairs={{0,3},{1,0},{2,1},{3,2},{4,7},{5,4},{6,5},{7,6},{8,11},{9,8},{10,9... | collective-permute-start | bytes 786440 | tf_op jit(solution)/shard_map/ppermute | solution.py:643
  452.0 3.9 collective-permute-start.41
  453.1 57.9 %collective-permute-start.48 = (bf16[6,256,128]{2,1,0:T(8,128)(2,1)}, bf16[6,256,128]{2,1,0:T(8,128)(2,1)}, u32[]{:S(2)}, u32[]{:S(2)}) collective-permute-start(bf16[6,256,128]{2,1,0:T(8,128)(2,1)} %get-tuple-element.367), channel_id=1, source_target_pairs={{0,1},{1,2},{2,3},{3,0},{4,5},{5,6},{6,7},{7,4},{8,9},{9,10},{10,1... | collective-permute-start | bytes 1179656 | tf_op jit(solution)/shard_map/ppermute | solution.py:643
  453.7 57.3 %collective-permute-start.49 = (bf16[6,256,128]{2,1,0:T(8,128)(2,1)}, bf16[6,256,128]{2,1,0:T(8,128)(2,1)}, u32[]{:S(2)}, u32[]{:S(2)}) collective-permute-start(bf16[6,256,128]{2,1,0:T(8,128)(2,1)} %get-tuple-element.369), channel_id=1, source_target_pairs={{0,2},{1,3},{2,0},{3,1},{4,6},{5,7},{6,4},{7,5},{8,10},{9,11},{10,... | collective-permute-start | bytes 1179656 | tf_op jit(solution)/shard_map/ppermute | solution.py:643
  455.9 55.1 %collective-permute-start.50 = (bf16[6,256,128]{2,1,0:T(8,128)(2,1)}, bf16[6,256,128]{2,1,0:T(8,128)(2,1)}, u32[]{:S(2)}, u32[]{:S(2)}) collective-permute-start(bf16[6,256,128]{2,1,0:T(8,128)(2,1)} %get-tuple-element.368), channel_id=1, source_target_pairs={{0,3},{1,0},{2,1},{3,2},{4,7},{5,4},{6,5},{7,6},{8,11},{9,8},{10,9... | collective-permute-start | bytes 1179656 | tf_op jit(solution)/shard_map/ppermute | solution.py:643
  464.8 4.6 collective-permute-start.43
  469.4 38.8 %collective-permute-start.38 = (bf16[2,128,640]{2,1,0:T(8,128)(2,1)S(1)}, bf16[2,128,640]{2,1,0:T(8,128)(2,1)S(1)}, u32[]{:S(2)}, u32[]{:S(2)}) collective-permute-start(bf16[2,128,640]{2,1,0:T(8,128)(2,1)S(1)} %dynamic-slice_bitcast_fusion.2), channel_id=1, source_target_pairs={{0,8},{4,12},{8,0},{12,4},{16,24},{20,28},{24,16},{28,20},{1,9},{5... | collective-permute-start | bytes 983048 | tf_op jit(solution)/shard_map/ppermute | solution.py:648
  471.6 10.1 %collective-permute-start.45 = (f32[92,128]{1,0:T(8,128)S(1)}, f32[92,128]{1,0:T(8,128)S(1)}, u32[]{:S(2)}, u32[]{:S(2)}) collective-permute-start(f32[92,128]{1,0:T(8,128)S(1)} %add.263), channel_id=1, source_target_pairs={{0,16},{4,20},{8,24},{12,28},{16,0},{20,4},{24,8},{28,12},{1,17},{... | collective-permute-start | bytes 141320 | tf_op jit(solution)/shard_map/ppermute | solution.py:648
  481.7 19.2 %collective-permute-start.46 = (f32[92,128]{1,0:T(8,128)S(1)}, f32[92,128]{1,0:T(8,128)S(1)}, u32[]{:S(2)}, u32[]{:S(2)}) collective-permute-start(f32[92,128]{1,0:T(8,128)S(1)} %add.264), channel_id=1, source_target_pairs={{0,1},{1,0},{2,3},{3,2},{4,5},{5,4},{6,7},{7,6},{8,9},{9,8},{10,11... | collective-permute-start | bytes 141320 | tf_op jit(solution)/shard_map/ppermute | solution.py:648
  501.0 5.4 %collective-permute-start.47 = (f32[92,128]{1,0:T(8,128)S(1)}, f32[92,128]{1,0:T(8,128)S(1)}, u32[]{:S(2)}, u32[]{:S(2)}) collective-permute-start(f32[92,128]{1,0:T(8,128)S(1)} %add.265), channel_id=1, source_target_pairs={{0,2},{1,3},{2,0},{3,1},{4,6},{5,7},{6,4},{7,5},{8,10},{9,11},{10,... | collective-permute-start | bytes 141320 | tf_op jit(solution)/shard_map/ppermute | solution.py:648
  506.4 3.5 collective-permute-start.52
  508.3 6.7 %collective-permute-start.39 = (bf16[128,640]{1,0:T(8,128)(2,1)S(1)}, bf16[128,640]{1,0:T(8,128)(2,1)S(1)}, u32[]{:S(2)}, u32[]{:S(2)}) collective-permute-start(bf16[128,640]{1,0:T(8,128)(2,1)S(1)} %dynamic-slice_bitcast_fusion.6), channel_id=1, source_target_pairs={{0,16},{4,20},{8,24},{12,28},{16,0},{20,4},{24,8},{28,12},{1,17},{... | collective-permute-start | bytes 491528 | tf_op jit(solution)/shard_map/ppermute | solution.py:648
  512.5 4.6 collective-permute-start.51
  (33 other events, 157.0 us)
Sparse Core Ops, SparseCore 0:
  67.8 156.4 all-gather.4
  234.1 66.0 all-gather.6
  303.2 54.8 reduce-scatter.6
  360.9 85.4 reduce-scatter.8
